TPU v7x, 32 devices: a whole 2x2x4 slice. The times are simulated.
32 devices in a mesh: groups: 2 (over x), blk: 4 (over y, core), ref: 4 (over z).
Axes of the slice: x: 2, y: 2, z: 4, core: 2. Of those that a mesh axis runs over, the one named last changes fastest.
Arguments:
- queries: bfloat16 [4096, 1024], P(('groups', 'blk')), parts along dimension 0, may hold values from -4 to 4
- references: bfloat16 [8192, 1024], P(('groups', 'blk', 'ref')), parts along dimension 0, may hold values from -4 to 4
- labels: bfloat16 [8192, 512], P(('groups', 'blk', 'ref')), parts along dimension 0, may hold values from 0.0009994507 to 1
Outputs:
- log_scores: float32 [4096, 512], P(('groups', 'blk', 'ref')), parts along dimension 0
There are 2 independent parts, one for each index of `groups`. A program takes and returns all parts, laid end to end along the dimension named above; each array names one. Nothing has to cross between parts.
All inputs are finite; a program needn't handle non-finite values.
Results may differ from a plain program's by a relative error of at most 0.007.
Values may be sent and summed in bfloat16 or wider, within the bound.
No kernel may reach another device: no remote copies, remote signals or barrier semaphores. Data moves between devices by JAX's collectives and lax.ppermute only.
A program may use at most 128 MiB of HBM per device.

v0:
```python
import math

import jax
import jax.numpy as jnp
from jax import lax
from jax.sharding import PartitionSpec as P

NEG_FLOOR = -1e30


def merged(value, axis, join):
    pieces = jax.tree.map(lambda part: lax.all_gather(part, axis), value)
    head = jax.tree.map(lambda part: part[0], pieces)
    tail = jax.tree.map(lambda part: part[1:], pieces)
    subtotal, _ = lax.scan(lambda subtotal, piece: (join(subtotal, piece), None), head, tail)
    return subtotal


def absorb(running, queries, ref_rows, label_rows, score_scale):
    row_top, row_total, row_mass = running
    scores = (
        lax.dot_general(
            queries, ref_rows, (((1,), (1,)), ((), ())), preferred_element_type=jnp.float32
        )
        * score_scale
    )
    new_top = jnp.maximum(row_top, jnp.max(scores, axis=1))
    shrink = jnp.exp(row_top - new_top)
    weights = jnp.exp(scores - new_top[:, None]).astype(jnp.bfloat16)
    row_total = row_total * shrink + jnp.sum(weights.astype(jnp.float32), axis=1)
    row_mass = row_mass * shrink[:, None] + jnp.dot(
        weights, label_rows, preferred_element_type=jnp.float32
    )
    return (new_top, row_total, row_mass)


def combine(first, second):
    new_top = jnp.maximum(first[0], second[0])
    scale_first = jnp.exp(first[0] - new_top)
    scale_second = jnp.exp(second[0] - new_top)
    row_total = first[1] * scale_first + second[1] * scale_second
    row_mass = first[2] * scale_first[:, None] + second[2] * scale_second[:, None]
    return (new_top, row_total, row_mass)


def per_device(queries, references, labels):
    width = queries.shape[1]
    classes = labels.shape[1]
    query_rows = queries.shape[0]
    score_scale = 2.0 / math.sqrt(width)
    initial = (
        jnp.full((query_rows,), NEG_FLOOR, jnp.float32),
        jnp.zeros((query_rows,), jnp.float32),
        jnp.zeros((query_rows, classes), jnp.float32),
    )
    running = initial
    ref_part = lax.all_gather(references, "blk", axis=0, tiled=True)
    label_part = lax.all_gather(labels, "blk", axis=0, tiled=True)
    count = ref_part.shape[0]
    span = math.gcd(count, 512)
    grouped_refs = ref_part.reshape(count // span, span, width)
    grouped_labels = label_part.reshape(count // span, span, classes)

    def advance(current, members):
        return (absorb(current, queries, members[0], members[1], score_scale), None)

    running, unused = lax.scan(advance, running, (grouped_refs, grouped_labels))
    row_top, row_total, row_mass = running
    share = query_rows // lax.axis_size("ref")
    row_top, row_total, row_mass = merged((row_top, row_total, row_mass), "ref", combine)
    offset = lax.axis_index("ref") * share
    mass_rows = lax.dynamic_slice_in_dim(row_mass, offset, share, 0)
    total_rows = lax.dynamic_slice_in_dim(row_total, offset, share, 0)
    return jnp.log(mass_rows) - jnp.log(total_rows)[:, None]


def solution(mesh):
    return jax.shard_map(
        per_device,
        mesh=mesh,
        in_specs=(
            P(("groups", "blk"), None),
            P(("groups", "blk", "ref"), None),
            P(("groups", "blk", "ref"), None),
        ),
        out_specs=P(("groups", "blk", "ref"), None),
        check_vma=False,
    )
```

profile of v0, /device:TPU:0, one launch (start us, length us, event | category | flops | bytes accessed | tf_op | source)
XLA Modules:
  0.0 158.2 jit_solution(7280220137814239432)
XLA Ops:
  6.5 0.7 all-gather.11.cloned.1.call-update
  7.3 0.7 all-gather.9.cloned.1.call-update
  8.0 0.0 all-gather.13.cloned.1.call-start
  8.1 20.3 %all-gather.11.cloned.1.call-done = bf16[1024,512]{1,0:T(8,128)(2,1)} async-done(((bf16[256,512]{1,0:T(8,128)(2,1)}), bf16[1024,512]{1,0:T(8,128)(2,1)}) %all-gather.11.cloned.1.call-update) | async-done | bytes 1048592 | tf_op jit(solution)/shard_map/all_gather | solution.py:58
  28.3 24.2 %all-gather.9.cloned.1.call-done = bf16[1024,1024]{1,0:T(8,128)(2,1)} async-done(((bf16[256,1024]{1,0:T(8,128)(2,1)}), bf16[1024,1024]{1,0:T(8,128)(2,1)}) %all-gather.9.cloned.1.call-update) | async-done | bytes 2097168 | tf_op jit(solution)/shard_map/all_gather | solution.py:57
  52.5 6.3 %while.30 = (s32[]{:T(128)}, f32[512]{0:T(512)S(1)}, f32[512]{0:T(512)S(1)}, f32[512,512]{1,0:T(8,128)S(1)}, bf16[2,512,1024]{2,1,0:T(8,128)(2,1)}, /*index=5*/b...) while((s32[]{:T(128)}, f32[512]{0:T(512)S(1)}, f32[512]{0:T(512)S(1)}, ...), condition=%wide.region_3.4_spmd.clone, body=%wide.region_0.3_spmd.clone.sunk | while | flops 808192512 | bytes 12092041 | solution.py:67
  52.5 2.4 %fusion.18 = (f32[512]{0:T(512)S(1)}, f32[512,512]{1,0:T(8,128)S(1)}) fusion(bf16[512,1024]{1,0:T(8,128)(2,1)} %get-tuple-element.278, bf16[2,512,1024]{2,1,0:T(8,128)(2,1)} %get-tuple-element.277, s32[]{:T(128)} %get-tuple-element.264), kind=kOutput, calls=%fused_computation.26.clone.1 | convolution fusion | flops 537394688 | bytes 3148288 | tf_op jit(solution)/shard_map/while/body/eval_jaxpr/dot_general | solution.py:22
  54.9 0.2 convert_reduce_fusion.2
  55.1 0.5 convolution_add_fusion.2
  55.7 2.4 %fusion.18 = (f32[512]{0:T(512)S(1)}, f32[512,512]{1,0:T(8,128)S(1)}) fusion(bf16[512,1024]{1,0:T(8,128)(2,1)} %get-tuple-element.278, bf16[2,512,1024]{2,1,0:T(8,128)(2,1)} %get-tuple-element.277, s32[]{:T(128)} %get-tuple-element.264), kind=kOutput, calls=%fused_computation.26.clone.1 | convolution fusion | flops 537394688 | bytes 3148288 | tf_op jit(solution)/shard_map/while/body/eval_jaxpr/dot_general | solution.py:22
  58.1 0.2 convert_reduce_fusion.2
  58.3 0.5 convolution_add_fusion.2
  58.8 1.0 copy-done
  59.8 12.0 %all-gather.3 = f32[4,1,512]{2,1,0:T(1,128)S(1)} all-gather(f32[1,1,512]{2,1,0:T(1,128)S(1)} %bitcast.42), channel_id=2, replica_groups=mesh['groups'=2,'blk'=4,'ref'=4] {'ref'}, dimensions={0}, use_global_device_ids=true | all-gather | bytes 10240 | tf_op jit(solution)/shard_map/all_gather | solution.py:12
  71.8 12.4 %all-gather.4 = f32[4,1,512]{2,1,0:T(1,128)S(1)} all-gather(f32[1,1,512]{2,1,0:T(1,128)S(1)} %bitcast.45), channel_id=3, replica_groups=mesh['groups'=2,'blk'=4,'ref'=4] {'ref'}, dimensions={0}, use_global_device_ids=true | all-gather | bytes 10240 | tf_op jit(solution)/shard_map/all_gather | solution.py:12
  84.3 56.6 %all-gather.13.cloned.1.call-done = f32[2048,512]{1,0:T(8,128)} async-done(((f32[512,512]{1,0:T(8,128)}), f32[2048,512]{1,0:T(8,128)}) %all-gather.13.cloned.1.call-update) | async-done | bytes 4194320 | tf_op jit(solution)/shard_map/all_gather | solution.py:12
  140.9 3.9 %slice.39 = f32[1536,512]{1,0:T(8,128)} slice(f32[2048,512]{1,0:T(8,128)} %all-gather.13.cloned.1.call-done), slice={[512:2048], [0:512]} | slice | bytes 6291456 | tf_op jit(solution)/shard_map/slice | solution.py:14
  144.7 1.3 slice.36
  146.0 4.7 %while.29 = (s32[]{:T(128)}, f32[512]{0:T(512)S(1)}, f32[512]{0:T(512)S(1)}, f32[512,512]{1,0:T(8,128)S(1)}, f32[3,512]{1,0:T(4,128)S(1)}, /*index=5*/f32[3,512]{1,0:T(4,128)S(1)}, f32[3,512,512]{2,1,0:T(8,128)}, s32[]{:T(128)}) while((s32[]{:T(128)}, f32[512]{0:T(512)S(1)}, f32[512]{0:T(512)S(1)}, f32[512,512]{1,0:T(8,128)S(1)}, ...), condition=%wide.region_5.6_spmd, body=%wide.region_4.5_spmd.sunk | while | flops 789506 | bytes 3174493 | solution.py:15
  146.1 1.5 fusion.15
  147.6 1.5 fusion.15
  149.2 1.5 fusion.15
  150.8 0.1 dynamic-slice_log_fusion
  150.8 0.8 log_subtract_fusion
  (29 shorter events, 0.2 us)
Async XLA Ops:
  6.5 21.8 %all-gather.11.cloned.1.call-start = ((), (), s32[]{:S(2)}) async-start(), calls=%async_computation.1 | async-start | bytes 1310720 | tf_op jit(solution)/shard_map/all_gather | solution.py:58
  7.3 45.2 %all-gather.9.cloned.1.call-start = ((), (), s32[]{:S(2)}) async-start(), calls=%async_computation | async-start | bytes 2621440 | tf_op jit(solution)/shard_map/all_gather | solution.py:57
  8.0 132.8 %all-gather.13.cloned.1.call-start = ((), (), s32[]{:S(2)}) async-start(), calls=%async_computation.2 | async-start | bytes 5242880 | tf_op jit(solution)/shard_map/all_gather | solution.py:12
  52.5 2.6 %copy-start.1 = (bf16[2,512,512]{2,1,0:T(8,128)(2,1)S(1)}, bf16[2,512,512]{2,1,0:T(8,128)(2,1)}, u32[]{:S(2)}) copy-start(bf16[2,512,512]{2,1,0:T(8,128)(2,1)} %get-tuple-element.279) | copy-start | bytes 3145732 | tf_op jit(solution)/shard_map/while
  55.7 2.6 %copy-start.1 = (bf16[2,512,512]{2,1,0:T(8,128)(2,1)S(1)}, bf16[2,512,512]{2,1,0:T(8,128)(2,1)}, u32[]{:S(2)}) copy-start(bf16[2,512,512]{2,1,0:T(8,128)(2,1)} %get-tuple-element.279) | copy-start | bytes 3145732 | tf_op jit(solution)/shard_map/while
  58.8 1.0 copy-start
Sparse Core Ops, SparseCore 0:
  8.9 19.4 all-gather.10
  29.9 22.5 all-gather.8
  60.0 80.8 all-gather.12
where the time goes:
time: 159 us; the launch traced here: 158 us
  waiting for transfers between devices  102 us (64%)
  blocking collectives  24.4 us (15%)
  between operations  13.2 us (8%)
  local copies, waits for them, and re-layouts  6.26 us (4%)
  other arithmetic  5.86 us (4%)
  matrix products  5.78 us (4%)
    all_gather x1, waiting for transfers between devices, merged(): pieces = jax.tree.map(lambda part: lax.all_gather(part, axis), value)  56.6 us
    all_gather x2, blocking collectives, merged(): pieces = jax.tree.map(lambda part: lax.all_gather(part, axis), value)  24.4 us
    all_gather x1, waiting for transfers between devices, per_device(): ref_part = lax.all_gather(references, 'blk', axis=0, tiled=True)  24.2 us
    all_gather x1, waiting for transfers between devices, per_device(): label_part = lax.all_gather(labels, 'blk', axis=0, tiled=True)  20.3 us
    dot_general x2, matrix products, absorb(): lax.dot_general(queries, ref_rows, (((1,), (1,)), ((), ())), preferred_el...  4.77 us
    add x3, other arithmetic, combine(): first[2] * scale_first[:, None] + second[2] * scale_second[:, None]  4.56 us
    slice x3, local copies, waits for them, and re-layouts, merged(): tail = jax.tree.map(lambda part: part[1:], pieces)  3.87 us
  transfers between devices with their start and end apart: 3, of which 3 were waited for; matrix products, arithmetic and copies ran while one was open for 0% of the time, Pallas kernels for 0%

commit v1 on v0

--- a/solution.py
+++ b/solution.py
@@ -3,6 +3,8 @@
 import jax
 import jax.numpy as jnp
 from jax import lax
+from jax.experimental import pallas as pl
+from jax.experimental.pallas import tpu as pltpu
 from jax.sharding import PartitionSpec as P
 
 NEG_FLOOR = -1e30
@@ -43,7 +45,7 @@
     return (new_top, row_total, row_mass)
 
 
-def per_device(queries, references, labels):
+def plain(queries, references, labels):
     width = queries.shape[1]
     classes = labels.shape[1]
     query_rows = queries.shape[0]
@@ -72,6 +74,256 @@
     mass_rows = lax.dynamic_slice_in_dim(row_mass, offset, share, 0)
     total_rows = lax.dynamic_slice_in_dim(row_total, offset, share, 0)
     return jnp.log(mass_rows) - jnp.log(total_rows)[:, None]
+
+
+LANES = 128
+STAT_ROWS = 16
+GRANT = 24 << 20
+BF16 = jnp.bfloat16
+F32 = jnp.float32
+VMEM = pl.BlockSpec(memory_space=pltpu.VMEM)
+SMEM = pl.BlockSpec(memory_space=pltpu.SMEM)
+
+
+def call(kernel, outs, in_specs, flops, name):
+    shapes = [jax.ShapeDtypeStruct(shape, dtype) for shape, dtype in outs]
+    moved = sum(math.prod(shape) * jnp.dtype(dtype).itemsize for shape, dtype in outs)
+    return pl.pallas_call(
+        kernel,
+        out_shape=shapes,
+        in_specs=in_specs,
+        out_specs=[VMEM] * len(shapes),
+        cost_estimate=pl.CostEstimate(flops=flops, bytes_accessed=moved, transcendentals=0),
+        compiler_params=pltpu.CompilerParams(vmem_limit_bytes=GRANT),
+        name=name,
+    )
+
+
+def swapped(value, axis, bit):
+    return lax.ppermute(value, axis, [(i, i ^ bit) for i in range(lax.axis_size(axis))])
+
+
+def scored(ref_rows, queries):
+    scale = 2.0 / math.sqrt(queries.shape[1])
+    return (
+        lax.dot_general(
+            ref_rows, queries, (((1,), (1,)), ((), ())), preferred_element_type=F32
+        )
+        * scale
+    )
+
+
+def even_top(top):
+    return top.astype(BF16).astype(F32)
+
+
+def arrange_kernel(place_ref, queries_ref, labels_ref, ordered_ref, upper_ref, lower_ref):
+    share = LANES
+    place = place_ref[0]
+    for block in range(queries_ref.shape[0] // share):
+        first = pl.multiple_of((place ^ block) * share, share)
+        ordered_ref[block * share : (block + 1) * share, :] = queries_ref[pl.ds(first, share), :]
+    half = labels_ref.shape[1] // 2
+    upper_ref[...] = labels_ref[:, :half].T
+    lower_ref[...] = labels_ref[:, half:].T
+
+
+def own_kernel(queries_ref, refs_a, refs_b, up_a, up_b, low_a, low_b, upper_ref, lower_ref, stat_ref):
+    queries = queries_ref[...]
+    scores_a = scored(refs_a[...], queries)
+    scores_b = scored(refs_b[...], queries)
+    top = jnp.maximum(
+        jnp.max(scores_a, axis=0, keepdims=True), jnp.max(scores_b, axis=0, keepdims=True)
+    )
+    top = even_top(top)
+    weights_a = jnp.exp(scores_a - top).astype(BF16)
+    weights_b = jnp.exp(scores_b - top).astype(BF16)
+    total = jnp.sum(weights_a.astype(F32), axis=0, keepdims=True) + jnp.sum(
+        weights_b.astype(F32), axis=0, keepdims=True
+    )
+    for out, first, second in ((upper_ref, up_a, up_b), (lower_ref, low_a, low_b)):
+        out[...] = jnp.dot(first[...], weights_a, preferred_element_type=F32) + jnp.dot(
+            second[...], weights_b, preferred_element_type=F32
+        )
+    stat_ref[0:1, :] = top
+    stat_ref[1:2, :] = total
+
+
+def score_kernel(queries_ref, refs_ref, scores_ref):
+    scores_ref[...] = scored(refs_ref[...], queries_ref[...])
+
+
+def weight_kernel(queries_ref, refs_ref, scores_ref, stat_ref, weights_ref, out_ref):
+    scores_a = scores_ref[...]
+    scores_b = scored(refs_ref[...], queries_ref[...])
+    rows = scores_a.shape[0]
+    top = jnp.maximum(
+        jnp.max(scores_a, axis=0, keepdims=True), jnp.max(scores_b, axis=0, keepdims=True)
+    )
+    own_top = stat_ref[0:1, :]
+    top = jnp.maximum(even_top(top), own_top)
+    weights_a = jnp.exp(scores_a - top).astype(BF16)
+    weights_b = jnp.exp(scores_b - top).astype(BF16)
+    weights_ref[:rows, :] = weights_a
+    weights_ref[rows:, :] = weights_b
+    shrink = jnp.exp(own_top - top)
+    total = (
+        stat_ref[1:2, :] * shrink
+        + jnp.sum(weights_a.astype(F32), axis=0, keepdims=True)
+        + jnp.sum(weights_b.astype(F32), axis=0, keepdims=True)
+    )
+    out_ref[0:1, :] = top
+    out_ref[1:2, :] = total
+    out_ref[2:3, :] = shrink
+
+
+def write_message(message_ref, columns, mass, top, total):
+    height = mass.shape[0]
+    high = total.astype(BF16)
+    low = (total - high.astype(F32)).astype(BF16)
+    message_ref[:height, columns] = mass.astype(BF16)
+    row = lax.broadcasted_iota(jnp.int32, (STAT_ROWS, mass.shape[1]), 0)
+    stats = jnp.where(
+        row == 0, top, jnp.where(row == 1, high.astype(F32), low.astype(F32))
+    )
+    message_ref[height:, columns] = stats.astype(BF16)
+
+
+def read_message(message_ref, columns):
+    height = message_ref.shape[0] - STAT_ROWS
+    mass = message_ref[:height, columns].astype(F32)
+    stats = message_ref[height:, columns].astype(F32)
+    return mass, stats[0:1], stats[1:2] + stats[2:3]
+
+
+def mass_kernel(label_a, label_b, weights_ref, own_ref, stat_ref, message_ref, keep_ref):
+    rows = label_a.shape[1]
+    mass = (
+        own_ref[...] * stat_ref[2:3, :]
+        + jnp.dot(label_a[...], weights_ref[:rows, :], preferred_element_type=F32)
+        + jnp.dot(label_b[...], weights_ref[rows:, :], preferred_element_type=F32)
+    )
+    for slot in range(2):
+        columns = slice(slot * LANES, (slot + 1) * LANES)
+        kept = slice(2 * slot * LANES, (2 * slot + 1) * LANES)
+        sent = slice((2 * slot + 1) * LANES, (2 * slot + 2) * LANES)
+        write_message(
+            message_ref, columns, mass[:, sent], stat_ref[0:1, sent], stat_ref[1:2, sent]
+        )
+        keep_ref[:, columns] = mass[:, kept]
+
+
+def joined(mass, top, total, other):
+    other_mass, other_top, other_total = other
+    new_top = jnp.maximum(top, other_top)
+    scale = jnp.exp(top - new_top)
+    other_scale = jnp.exp(other_top - new_top)
+    return (
+        mass * scale + other_mass * other_scale,
+        new_top,
+        total * scale + other_total * other_scale,
+    )
+
+
+def halve_kernel(received_ref, keep_ref, stat_ref, message_ref, out_ref, out_stat_ref):
+    near, far = slice(0, LANES), slice(LANES, 2 * LANES)
+    block = slice(2 * LANES, 3 * LANES)
+    mass, top, total = joined(
+        keep_ref[:, far], stat_ref[0:1, block], stat_ref[1:2, block], read_message(received_ref, far)
+    )
+    write_message(message_ref, slice(None), mass, top, total)
+    mass, top, total = joined(
+        keep_ref[:, near], stat_ref[0:1, near], stat_ref[1:2, near], read_message(received_ref, near)
+    )
+    out_ref[...] = mass
+    out_stat_ref[0:1, :] = top
+    out_stat_ref[1:2, :] = total
+
+
+def final_kernel(got_upper, got_lower, upper_ref, lower_ref, stat_ref, out_ref):
+    half = upper_ref.shape[0]
+    for part, (got, keep) in enumerate(((got_upper, upper_ref), (got_lower, lower_ref))):
+        mass, _, total = joined(
+            keep[...], stat_ref[0:1, :], stat_ref[1:2, :], read_message(got, slice(None))
+        )
+        out_ref[:, part * half : (part + 1) * half] = (jnp.log(mass) - jnp.log(total)).T
+
+
+def fits(queries, references, labels):
+    share = queries.shape[0] // lax.axis_size("ref")
+    return (
+        lax.axis_size("blk") == 4
+        and lax.axis_size("ref") == 4
+        and share == LANES
+        and labels.shape[1] % (2 * LANES) == 0
+        and references.shape[0] % LANES == 0
+    )
+
+
+def per_device(queries, references, labels):
+    if not fits(queries, references, labels):
+        return plain(queries, references, labels)
+    count, width = references.shape
+    rows, classes = queries.shape[0], labels.shape[1]
+    half = classes // 2
+    pair = 2 * LANES
+    score_flops = 2 * count * rows * width
+    mass_flops = 4 * count * rows * half
+
+    far_refs = swapped(references, "blk", 2)
+    mate_refs = swapped(references, "blk", 1)
+    place = lax.axis_index("ref").astype(jnp.int32).reshape(1)
+    ordered, upper, lower = call(
+        arrange_kernel,
+        [((rows, width), BF16), ((half, count), BF16), ((half, count), BF16)],
+        [SMEM, VMEM, VMEM],
+        0,
+        "arrange",
+    )(place, queries, labels)
+    far_labels = [swapped(part, "blk", 2) for part in (upper, lower)]
+    mate_labels = [swapped(part, "blk", 1) for part in (upper, lower)]
+    own_upper, own_lower, own_stat = call(
+        own_kernel,
+        [((half, rows), F32), ((half, rows), F32), ((8, rows), F32)],
+        [VMEM] * 7,
+        2 * score_flops + 2 * mass_flops,
+        "own",
+    )(ordered, references, mate_refs, upper, mate_labels[0], lower, mate_labels[1])
+    cross_refs = swapped(far_refs, "blk", 1)
+    cross_labels = [swapped(part, "blk", 1) for part in far_labels]
+    (scores,) = call(
+        score_kernel, [((count, rows), F32)], [VMEM] * 2, score_flops, "score"
+    )(ordered, far_refs)
+    weights, stat = call(
+        weight_kernel,
+        [((2 * count, rows), BF16), ((8, rows), F32)],
+        [VMEM] * 4,
+        score_flops,
+        "weight",
+    )(ordered, cross_refs, scores, own_stat)
+    got, kept = [], []
+    for own, far, cross in zip((own_upper, own_lower), far_labels, cross_labels):
+        message, keep = call(
+            mass_kernel,
+            [((half + STAT_ROWS, pair), BF16), ((half, pair), F32)],
+            [VMEM] * 5,
+            mass_flops,
+            "mass",
+        )(far, cross, weights, own, stat)
+        received = swapped(message, "ref", 1)
+        message, keep, near_stat = call(
+            halve_kernel,
+            [((half + STAT_ROWS, LANES), BF16), ((half, LANES), F32), ((8, LANES), F32)],
+            [VMEM] * 3,
+            0,
+            "halve",
+        )(received, keep, stat)
+        got.append(swapped(message, "ref", 2))
+        kept.append(keep)
+    (out,) = call(final_kernel, [((LANES, classes), F32)], [VMEM] * 5, 0, "final")(
+        *got, *kept, near_stat
+    )
+    return out
 
 
 def solution(mesh):

time: 159 us -> 46.6 us (0.29)
  waiting for transfers between devices: 102 us -> 25.1 us
  blocking collectives: 24.4 us -> 0 us
  starting transfers between devices: 0.08 us -> 13.5 us
  between operations: 13.2 us -> 0.09 us
  other arithmetic: 5.86 us -> 0 us
  matrix products: 5.78 us -> 0 us
  Pallas kernels: 0 us -> 4.91 us
  local copies, waits for them, and re-layouts: 6.26 us -> 2.72 us
    all_gather x3 -> x0, waiting for transfers between devices: 101 us -> none  [the longest x1 56.6 us: merged(): pieces = jax.tree.map(lambda part: lax.all_gather(part, axis), value)]
    ppermute x0 -> x13, waiting for transfers between devices: none -> 25.1 us  [swapped(): lax.ppermute(value, axis, [(i, i ^ bit) for i in range(lax.axis_size(axis...]
    all_gather x2 -> x0, blocking collectives: 24.4 us -> none  [merged(): pieces = jax.tree.map(lambda part: lax.all_gather(part, axis), value)]
    ppermute x0 -> x13, starting transfers between devices: none -> 13.5 us  [swapped(): lax.ppermute(value, axis, [(i, i ^ bit) for i in range(lax.axis_size(axis...]
    dot_general x4 -> x0, matrix products: 5.78 us -> none  [the longest x2 4.77 us: absorb(): lax.dot_general(queries, ref_rows, (((1,), (1,)), ((), ())), preferred_el...]
    slice x6 -> x0, local copies, waits for them, and re-layouts: 5.16 us -> none  [the longest x3 3.87 us: merged(): tail = jax.tree.map(lambda part: part[1:], pieces)]
    pallas_call x0 -> x9, Pallas kernels: none -> 4.91 us  [the longest x1 1.41 us: per_device(): call(own_kernel, [((half, rows), F32), ((half, rows), F32), ((8, rows), F...]
    add x8 -> x0, other arithmetic: 4.65 us -> none  [the longest x3 4.56 us: combine(): first[2] * scale_first[:, None] + second[2] * scale_second[:, None]]
  transfers between devices with their start and end apart: 3 -> 13, of which waited for: 3 -> 6; matrix products, arithmetic and copies ran while one was open for 0% -> 0% of each run, Pallas kernels for 0% -> 9%
where the time goes in v1:
time: 46.6 us; the launch traced here: 46.4 us
  waiting for transfers between devices  25.1 us (54%)
  starting transfers between devices  13.5 us (29%)
  Pallas kernels  4.91 us (11%)
  local copies, waits for them, and re-layouts  2.72 us (6%)
    ppermute x13, waiting for transfers between devices, swapped(): lax.ppermute(value, axis, [(i, i ^ bit) for i in range(lax.axis_size(axis...  25.1 us
    ppermute x13, starting transfers between devices, swapped(): lax.ppermute(value, axis, [(i, i ^ bit) for i in range(lax.axis_size(axis...  13.5 us
    unnamed x6, local copies, waits for them, and re-layouts  2.72 us
    pallas_call x1, Pallas kernels, per_device(): call(own_kernel, [((half, rows), F32), ((half, rows), F32), ((8, rows), F...  1.41 us
  transfers between devices with their start and end apart: 13, of which 6 were waited for; matrix products, arithmetic and copies ran while one was open for 0% of the time, Pallas kernels for 9%

profile of v1, /device:TPU:0, one launch (start us, length us, event | category | flops | bytes accessed | tf_op | source)
XLA Modules:
  0.0 46.4 jit_solution(8530667406058949478)
XLA Ops:
  0.0 3.0 %collective-permute-start.2 = (bf16[256,1024]{1,0:T(8,128)(2,1)}, bf16[256,1024]{1,0:T(8,128)(2,1)S(1)}, u32[]{:S(2)}, u32[]{:S(2)}) collective-permute-start(bf16[256,1024]{1,0:T(8,128)(2,1)} %refs_a.1), channel_id=1, source_target_pairs={{0,8},{4,12},{8,0},{12,4},{1,9},{5,13},{9,1},{13,5},{2,10},{6,14},... | collective-permute-start | bytes 1572872 | tf_op jit(solution)/shard_map/ppermute | solution.py:103
  3.0 12.1 %collective-permute-done.2.refs_ref = bf16[256,1024]{1,0:T(8,128)(2,1)S(1)} collective-permute-done((bf16[256,1024]{1,0:T(8,128)(2,1)}, bf16[256,1024]{1,0:T(8,128)(2,1)S(1)}, u32[]{:S(2)}, u32[]{:S(2)}) %collective-permute-start.2) | collective-permute-done | bytes 524320 | tf_op jit(solution)/shard_map/ppermute | solution.py:103
  15.1 1.2 %copy-done = bf16[512,1024]{1,0:T(8,128)(2,1)S(1)} copy-done((bf16[512,1024]{1,0:T(8,128)(2,1)S(1)}, bf16[512,1024]{1,0:T(8,128)(2,1)}, u32[]{:S(2)}) %copy-start) | copy-done | bytes 1048600
  16.4 0.9 %copy-done.1 = bf16[256,512]{1,0:T(8,128)(2,1)S(1)} copy-done((bf16[256,512]{1,0:T(8,128)(2,1)S(1)}, bf16[256,512]{1,0:T(8,128)(2,1)}, u32[]{:S(2)}) %copy-start.1) | copy-done | bytes 262168
  17.4 0.6 %collective-permute-start.5 = (bf16[256,256]{1,0:T(8,128)(2,1)S(1)}, bf16[256,256]{1,0:T(8,128)(2,1)S(1)}, u32[]{:S(2)}, u32[]{:S(2)}) collective-permute-start(bf16[256,256]{1,0:T(8,128)(2,1)S(1)} %get-tuple-element.22.up_a), channel_id=1, source_target_pairs={{0,4},{4,0},{8,12},{12,8},{1,5},{5,1},{9,13},{13,9},{2,6},{6,2},{1... | collective-permute-start | bytes 393224 | tf_op jit(solution)/shard_map/ppermute | solution.py:103
  18.0 1.7 %collective-permute-start.9 = (bf16[256,256]{1,0:T(8,128)(2,1)S(1)}, bf16[256,256]{1,0:T(8,128)(2,1)S(1)}, u32[]{:S(2)}, u32[]{:S(2)}) collective-permute-start(bf16[256,256]{1,0:T(8,128)(2,1)S(1)} %get-tuple-element.24.low_a), channel_id=1, source_target_pairs={{0,8},{4,12},{8,0},{12,4},{1,9},{5,13},{9,1},{13,5},{2,10},{6,14},... | collective-permute-start | bytes 393224 | tf_op jit(solution)/shard_map/ppermute | solution.py:103
  19.7 0.3 collective-permute-start
  20.0 4.3 %collective-permute-done.9.label_a = bf16[256,256]{1,0:T(8,128)(2,1)S(1)} collective-permute-done((bf16[256,256]{1,0:T(8,128)(2,1)S(1)}, bf16[256,256]{1,0:T(8,128)(2,1)S(1)}, u32[]{:S(2)}, u32[]{:S(2)}) %collective-permute-start.9) | collective-permute-done | bytes 131104 | tf_op jit(solution)/shard_map/ppermute | solution.py:103
  24.4 1.9 %collective-permute-done.label_a = bf16[256,256]{1,0:T(8,128)(2,1)S(1)} collective-permute-done((bf16[256,256]{1,0:T(8,128)(2,1)S(1)}, bf16[256,256]{1,0:T(8,128)(2,1)S(1)}, u32[]{:S(2)}, u32[]{:S(2)}) %collective-permute-start) | collective-permute-done | bytes 131104 | tf_op jit(solution)/shard_map/ppermute | solution.py:103
  26.3 0.5 %score.1.scores_ref = f32[256,512]{1,0:T(8,128)S(1)} custom-call(bf16[512,1024]{1,0:T(8,128)(2,1)S(1)} %get-tuple-element.23.queries_ref, bf16[256,1024]{1,0:T(8,128)(2,1)S(1)} %collective-permute-done.2.refs_ref), custom_call_target="tpu_custom_call" | custom-call | flops 268435456 | bytes 524288 | tf_op jit(solution)/shard_map/score/pallas_call | solution.py:294
  26.8 0.5 %copy-done.2 = bf16[256,1024]{1,0:T(8,128)(2,1)S(1)} copy-done((bf16[256,1024]{1,0:T(8,128)(2,1)S(1)}, bf16[256,1024]{1,0:T(8,128)(2,1)}, u32[]{:S(2)}) %copy-start.2) | copy-done | bytes 524312
  27.3 1.4 %own.1 = (f32[256,512]{1,0:T(8,128)S(1)}, f32[256,512]{1,0:T(8,128)S(1)}, f32[8,512]{1,0:T(8,128)S(1)}) custom-call(bf16[512,1024]{1,0:T(8,128)(2,1)S(1)} %get-tuple-element.23.queries_ref, bf16[256,1024]{1,0:T(8,128)(2,1)S(1)} %copy-done.2, bf16[256,1024]{1,0:T(8,128)(2,1)S(1)} %collective-permute-done.4.refs_b, ...), custom_call_target="tpu_custom_call" | custom-call | flops 805306368 | bytes 1064960 | tf_op jit(solution)/shard_map/own/pallas_call | solution.py:285
  28.8 0.8 %weight.1 = (bf16[512,512]{1,0:T(8,128)(2,1)S(1)}, f32[8,512]{1,0:T(8,128)S(1)}) custom-call(bf16[512,1024]{1,0:T(8,128)(2,1)S(1)} %get-tuple-element.23.queries_ref, bf16[256,1024]{1,0:T(8,128)(2,1)S(1)} %collective-permute-done.3.refs_ref, f32[256,512]{1,0:T(8,128)S(1)} %score.1.scores_ref, f32[8,512]{1,0:T(8,128)S(1)} %get-tuple-element.25.stat_ref), custom_call_target="tpu_custom_call" | custom-call | flops 268435456 | bytes 540672 | tf_op jit(solution)/shard_map/weight/pallas_call | solution.py:297
  29.6 0.3 mass.3
  29.9 1.9 %collective-permute-start.11 = (bf16[272,256]{1,0:T(8,128)(2,1)S(1)}, bf16[272,256]{1,0:T(8,128)(2,1)S(1)}, u32[]{:S(2)}, u32[]{:S(2)}) collective-permute-start(bf16[272,256]{1,0:T(8,128)(2,1)S(1)} %get-tuple-element.33), channel_id=1, source_target_pairs={{0,1},{1,0},{2,3},{3,2},{4,5},{5,4},{6,7},{7,6},{8,9},{9,8},{10,11... | collective-permute-start | bytes 417800 | tf_op jit(solution)/shard_map/ppermute | solution.py:103
  31.7 0.3 mass.2
  32.1 0.3 collective-permute-start.7
  32.3 4.1 %collective-permute-done.11.received_ref = bf16[272,256]{1,0:T(8,128)(2,1)S(1)} collective-permute-done((bf16[272,256]{1,0:T(8,128)(2,1)S(1)}, bf16[272,256]{1,0:T(8,128)(2,1)S(1)}, u32[]{:S(2)}, u32[]{:S(2)}) %collective-permute-start.11) | collective-permute-done | bytes 139296 | tf_op jit(solution)/shard_map/ppermute | solution.py:103
  36.5 2.9 %collective-permute-start.12 = (bf16[272,128]{1,0:T(8,128)(2,1)S(1)}, bf16[272,128]{1,0:T(8,128)(2,1)S(1)}, u32[]{:S(2)}, u32[]{:S(2)}) collective-permute-start(bf16[272,128]{1,0:T(8,128)(2,1)S(1)} %get-tuple-element.35), channel_id=1, source_target_pairs={{0,2},{1,3},{2,0},{3,1},{4,6},{5,7},{6,4},{7,5},{8,10},{9,11},{10,... | collective-permute-start | bytes 208904 | tf_op jit(solution)/shard_map/ppermute | solution.py:103
  39.4 0.6 %halve.2 = (bf16[272,128]{1,0:T(8,128)(2,1)S(1)}, f32[256,128]{1,0:T(8,128)S(1)}, f32[8,128]{1,0:T(8,128)}) custom-call(bf16[272,256]{1,0:T(8,128)(2,1)S(1)} %collective-permute-done.7.received_ref, f32[256,256]{1,0:T(8,128)S(1)} %get-tuple-element.30.keep_ref, f32[8,512]{1,0:T(8,128)S(1)} %get-tuple-element.28.stat_ref), custom_call_target="tpu_custom_call" | custom-call | bytes 204800 | tf_op jit(solution)/shard_map/halve/pallas_call | solution.py:314
  40.0 2.9 %collective-permute-start.8 = (bf16[272,128]{1,0:T(8,128)(2,1)S(1)}, bf16[272,128]{1,0:T(8,128)(2,1)S(1)}, u32[]{:S(2)}, u32[]{:S(2)}) collective-permute-start(bf16[272,128]{1,0:T(8,128)(2,1)S(1)} %get-tuple-element.31), channel_id=1, source_target_pairs={{0,2},{1,3},{2,0},{3,1},{4,6},{5,7},{6,4},{7,5},{8,10},{9,11},{10,... | collective-permute-start | bytes 208904 | tf_op jit(solution)/shard_map/ppermute | solution.py:103
  42.9 0.4 collective-permute-done.12.got_lower
  43.3 2.2 %collective-permute-done.8.got_upper = bf16[272,128]{1,0:T(8,128)(2,1)S(1)} collective-permute-done((bf16[272,128]{1,0:T(8,128)(2,1)S(1)}, bf16[272,128]{1,0:T(8,128)(2,1)S(1)}, u32[]{:S(2)}, u32[]{:S(2)}) %collective-permute-start.8) | collective-permute-done | bytes 69664 | tf_op jit(solution)/shard_map/ppermute | solution.py:103
  45.5 0.9 %final.1 = f32[128,512]{1,0:T(8,128)} custom-call(bf16[272,128]{1,0:T(8,128)(2,1)S(1)} %collective-permute-done.8.got_upper, bf16[272,128]{1,0:T(8,128)(2,1)S(1)} %collective-permute-done.12.got_lower, f32[256,128]{1,0:T(8,128)S(1)} %get-tuple-element.36.upper_ref, f32[256,128]{1,0:T(8,128)S(1)} %get-tuple-element.37.lower_ref, ...), custom_call_target="tpu_custom_call" | custom-call | bytes 262144 | tf_op jit(solution)/shard_map/final/pallas_call | solution.py:323
  (17 shorter events, 0.2 us)
Async XLA Ops:
  0.0 15.1 %collective-permute-start.2 = (bf16[256,1024]{1,0:T(8,128)(2,1)}, bf16[256,1024]{1,0:T(8,128)(2,1)S(1)}, u32[]{:S(2)}, u32[]{:S(2)}) collective-permute-start(bf16[256,1024]{1,0:T(8,128)(2,1)} %refs_a.1), channel_id=1, source_target_pairs={{0,8},{4,12},{8,0},{12,4},{1,9},{5,13},{9,1},{13,5},{2,10},{6,14},... | collective-permute-start | bytes 1572872 | tf_op jit(solution)/shard_map/ppermute | solution.py:103
  3.0 23.8 %collective-permute-start.4 = (bf16[256,1024]{1,0:T(8,128)(2,1)}, bf16[256,1024]{1,0:T(8,128)(2,1)S(1)}, u32[]{:S(2)}, u32[]{:S(2)}) collective-permute-start(bf16[256,1024]{1,0:T(8,128)(2,1)} %refs_a.1), channel_id=1, source_target_pairs={{0,4},{4,0},{8,12},{12,8},{1,5},{5,1},{9,13},{13,9},{2,6},{6,2},{1... | collective-permute-start | bytes 1572872 | tf_op jit(solution)/shard_map/ppermute | solution.py:103
  15.1 13.6 %collective-permute-start.3 = (bf16[256,1024]{1,0:T(8,128)(2,1)S(1)}, bf16[256,1024]{1,0:T(8,128)(2,1)S(1)}, u32[]{:S(2)}, u32[]{:S(2)}) collective-permute-start(bf16[256,1024]{1,0:T(8,128)(2,1)S(1)} %collective-permute-done.2.refs_ref), channel_id=1, source_target_pairs={{0,4},{4,0},{8,12},{12,8},{1,5},{5,1},{9,13},{13,9},{2,6},{6,2},{1... | collective-permute-start | bytes 1572872 | tf_op jit(solution)/shard_map/ppermute | solution.py:103
  15.1 1.2 %copy-start = (bf16[512,1024]{1,0:T(8,128)(2,1)S(1)}, bf16[512,1024]{1,0:T(8,128)(2,1)}, u32[]{:S(2)}) copy-start(bf16[512,1024]{1,0:T(8,128)(2,1)} %queries_ref.1) | copy-start | bytes 3145732
  16.4 0.9 %copy-start.1 = (bf16[256,512]{1,0:T(8,128)(2,1)S(1)}, bf16[256,512]{1,0:T(8,128)(2,1)}, u32[]{:S(2)}) copy-start(bf16[256,512]{1,0:T(8,128)(2,1)} %labels_ref.1) | copy-start | bytes 786436
  17.4 2.6 %collective-permute-start.5 = (bf16[256,256]{1,0:T(8,128)(2,1)S(1)}, bf16[256,256]{1,0:T(8,128)(2,1)S(1)}, u32[]{:S(2)}, u32[]{:S(2)}) collective-permute-start(bf16[256,256]{1,0:T(8,128)(2,1)S(1)} %get-tuple-element.22.up_a), channel_id=1, source_target_pairs={{0,4},{4,0},{8,12},{12,8},{1,5},{5,1},{9,13},{13,9},{2,6},{6,2},{1... | collective-permute-start | bytes 393224 | tf_op jit(solution)/shard_map/ppermute | solution.py:103
  18.0 6.4 %collective-permute-start.9 = (bf16[256,256]{1,0:T(8,128)(2,1)S(1)}, bf16[256,256]{1,0:T(8,128)(2,1)S(1)}, u32[]{:S(2)}, u32[]{:S(2)}) collective-permute-start(bf16[256,256]{1,0:T(8,128)(2,1)S(1)} %get-tuple-element.24.low_a), channel_id=1, source_target_pairs={{0,8},{4,12},{8,0},{12,4},{1,9},{5,13},{9,1},{13,5},{2,10},{6,14},... | collective-permute-start | bytes 393224 | tf_op jit(solution)/shard_map/ppermute | solution.py:103
  19.7 6.5 %collective-permute-start = (bf16[256,256]{1,0:T(8,128)(2,1)S(1)}, bf16[256,256]{1,0:T(8,128)(2,1)S(1)}, u32[]{:S(2)}, u32[]{:S(2)}) collective-permute-start(bf16[256,256]{1,0:T(8,128)(2,1)S(1)} %get-tuple-element.22.up_a), channel_id=1, source_target_pairs={{0,8},{4,12},{8,0},{12,4},{1,9},{5,13},{9,1},{13,5},{2,10},{6,14},... | collective-permute-start | bytes 393224 | tf_op jit(solution)/shard_map/ppermute | solution.py:103
  20.0 6.7 %collective-permute-start.6 = (bf16[256,256]{1,0:T(8,128)(2,1)S(1)}, bf16[256,256]{1,0:T(8,128)(2,1)S(1)}, u32[]{:S(2)}, u32[]{:S(2)}) collective-permute-start(bf16[256,256]{1,0:T(8,128)(2,1)S(1)} %get-tuple-element.24.low_a), channel_id=1, source_target_pairs={{0,4},{4,0},{8,12},{12,8},{1,5},{5,1},{9,13},{13,9},{2,6},{6,2},{1... | collective-permute-start | bytes 393224 | tf_op jit(solution)/shard_map/ppermute | solution.py:103
  24.4 5.2 %collective-permute-start.10 = (bf16[256,256]{1,0:T(8,128)(2,1)S(1)}, bf16[256,256]{1,0:T(8,128)(2,1)S(1)}, u32[]{:S(2)}, u32[]{:S(2)}) collective-permute-start(bf16[256,256]{1,0:T(8,128)(2,1)S(1)} %collective-permute-done.9.label_a), channel_id=1, source_target_pairs={{0,4},{4,0},{8,12},{12,8},{1,5},{5,1},{9,13},{13,9},{2,6},{6,2},{1... | collective-permute-start | bytes 393224 | tf_op jit(solution)/shard_map/ppermute | solution.py:103
  26.3 5.4 %collective-permute-start.1 = (bf16[256,256]{1,0:T(8,128)(2,1)S(1)}, bf16[256,256]{1,0:T(8,128)(2,1)S(1)}, u32[]{:S(2)}, u32[]{:S(2)}) collective-permute-start(bf16[256,256]{1,0:T(8,128)(2,1)S(1)} %collective-permute-done.label_a), channel_id=1, source_target_pairs={{0,4},{4,0},{8,12},{12,8},{1,5},{5,1},{9,13},{13,9},{2,6},{6,2},{1... | collective-permute-start | bytes 393224 | tf_op jit(solution)/shard_map/ppermute | solution.py:103
  26.3 1.0 %copy-start.2 = (bf16[256,1024]{1,0:T(8,128)(2,1)S(1)}, bf16[256,1024]{1,0:T(8,128)(2,1)}, u32[]{:S(2)}) copy-start(bf16[256,1024]{1,0:T(8,128)(2,1)} %refs_a.1) | copy-start | bytes 1572868
  29.9 6.6 %collective-permute-start.11 = (bf16[272,256]{1,0:T(8,128)(2,1)S(1)}, bf16[272,256]{1,0:T(8,128)(2,1)S(1)}, u32[]{:S(2)}, u32[]{:S(2)}) collective-permute-start(bf16[272,256]{1,0:T(8,128)(2,1)S(1)} %get-tuple-element.33), channel_id=1, source_target_pairs={{0,1},{1,0},{2,3},{3,2},{4,5},{5,4},{6,7},{7,6},{8,9},{9,8},{10,11... | collective-permute-start | bytes 417800 | tf_op jit(solution)/shard_map/ppermute | solution.py:103
  32.1 7.4 %collective-permute-start.7 = (bf16[272,256]{1,0:T(8,128)(2,1)S(1)}, bf16[272,256]{1,0:T(8,128)(2,1)S(1)}, u32[]{:S(2)}, u32[]{:S(2)}) collective-permute-start(bf16[272,256]{1,0:T(8,128)(2,1)S(1)} %get-tuple-element.29), channel_id=1, source_target_pairs={{0,1},{1,0},{2,3},{3,2},{4,5},{5,4},{6,7},{7,6},{8,9},{9,8},{10,11... | collective-permute-start | bytes 417800 | tf_op jit(solution)/shard_map/ppermute | solution.py:103
  36.5 6.7 %collective-permute-start.12 = (bf16[272,128]{1,0:T(8,128)(2,1)S(1)}, bf16[272,128]{1,0:T(8,128)(2,1)S(1)}, u32[]{:S(2)}, u32[]{:S(2)}) collective-permute-start(bf16[272,128]{1,0:T(8,128)(2,1)S(1)} %get-tuple-element.35), channel_id=1, source_target_pairs={{0,2},{1,3},{2,0},{3,1},{4,6},{5,7},{6,4},{7,5},{8,10},{9,11},{10,... | collective-permute-start | bytes 208904 | tf_op jit(solution)/shard_map/ppermute | solution.py:103
  40.0 5.5 %collective-permute-start.8 = (bf16[272,128]{1,0:T(8,128)(2,1)S(1)}, bf16[272,128]{1,0:T(8,128)(2,1)S(1)}, u32[]{:S(2)}, u32[]{:S(2)}) collective-permute-start(bf16[272,128]{1,0:T(8,128)(2,1)S(1)} %get-tuple-element.31), channel_id=1, source_target_pairs={{0,2},{1,3},{2,0},{3,1},{4,6},{5,7},{6,4},{7,5},{8,10},{9,11},{10,... | collective-permute-start | bytes 208904 | tf_op jit(solution)/shard_map/ppermute | solution.py:103

commit v2 on v1

--- a/solution.py
+++ b/solution.py
@@ -1,3 +1,4 @@
+import functools
 import math
 
 import jax
@@ -6,6 +7,7 @@
 from jax.experimental import pallas as pl
 from jax.experimental.pallas import tpu as pltpu
 from jax.sharding import PartitionSpec as P
+
 
 NEG_FLOOR = -1e30
 
@@ -66,7 +68,7 @@
     def advance(current, members):
         return (absorb(current, queries, members[0], members[1], score_scale), None)
 
-    running, unused = lax.scan(advance, running, (grouped_refs, grouped_labels))
+    running, _ = lax.scan(advance, running, (grouped_refs, grouped_labels))
     row_top, row_total, row_mass = running
     share = query_rows // lax.axis_size("ref")
     row_top, row_total, row_mass = merged((row_top, row_total, row_mass), "ref", combine)
@@ -78,6 +80,7 @@
 
 LANES = 128
 STAT_ROWS = 16
+CUTS = (0, 256, 512)
 GRANT = 24 << 20
 BF16 = jnp.bfloat16
 F32 = jnp.float32
@@ -85,7 +88,7 @@
 SMEM = pl.BlockSpec(memory_space=pltpu.SMEM)
 
 
-def call(kernel, outs, in_specs, flops, name):
+def call(kernel, outs, in_specs, flops):
     shapes = [jax.ShapeDtypeStruct(shape, dtype) for shape, dtype in outs]
     moved = sum(math.prod(shape) * jnp.dtype(dtype).itemsize for shape, dtype in outs)
     return pl.pallas_call(
@@ -95,7 +98,6 @@
         out_specs=[VMEM] * len(shapes),
         cost_estimate=pl.CostEstimate(flops=flops, bytes_accessed=moved, transcendentals=0),
         compiler_params=pltpu.CompilerParams(vmem_limit_bytes=GRANT),
-        name=name,
     )
 
 
@@ -117,18 +119,24 @@
     return top.astype(BF16).astype(F32)
 
 
-def arrange_kernel(place_ref, queries_ref, labels_ref, ordered_ref, upper_ref, lower_ref):
+def arrange_kernel(cuts, place_ref, queries_ref, labels_ref, ordered_ref, *label_refs):
     share = LANES
     place = place_ref[0]
+    for first, last, label_ref in zip(cuts, cuts[1:], label_refs):
+        label_ref[...] = labels_ref[:, first:last].T
     for block in range(queries_ref.shape[0] // share):
         first = pl.multiple_of((place ^ block) * share, share)
         ordered_ref[block * share : (block + 1) * share, :] = queries_ref[pl.ds(first, share), :]
-    half = labels_ref.shape[1] // 2
-    upper_ref[...] = labels_ref[:, :half].T
-    lower_ref[...] = labels_ref[:, half:].T
-
-
-def own_kernel(queries_ref, refs_a, refs_b, up_a, up_b, low_a, low_b, upper_ref, lower_ref, stat_ref):
+
+
+def own_kernel(queries_ref, refs_a, refs_b, *refs):
+    parts = (len(refs) - 1) // 3
+    labels_a, labels_b, masses, stat_ref = (
+        refs[:parts],
+        refs[parts : 2 * parts],
+        refs[2 * parts : 3 * parts],
+        refs[-1],
+    )
     queries = queries_ref[...]
     scores_a = scored(refs_a[...], queries)
     scores_b = scored(refs_b[...], queries)
@@ -141,7 +149,7 @@
     total = jnp.sum(weights_a.astype(F32), axis=0, keepdims=True) + jnp.sum(
         weights_b.astype(F32), axis=0, keepdims=True
     )
-    for out, first, second in ((upper_ref, up_a, up_b), (lower_ref, low_a, low_b)):
+    for out, first, second in zip(masses, labels_a, labels_b):
         out[...] = jnp.dot(first[...], weights_a, preferred_element_type=F32) + jnp.dot(
             second[...], weights_b, preferred_element_type=F32
         )
@@ -240,13 +248,17 @@
     out_stat_ref[1:2, :] = total
 
 
-def final_kernel(got_upper, got_lower, upper_ref, lower_ref, stat_ref, out_ref):
-    half = upper_ref.shape[0]
-    for part, (got, keep) in enumerate(((got_upper, upper_ref), (got_lower, lower_ref))):
+def final_kernel(stat_ref, *refs):
+    parts = len(refs) // 2
+    got, kept, out_ref = refs[:parts], refs[parts : 2 * parts], refs[-1]
+    first = 0
+    for message_ref, keep_ref in zip(got, kept):
+        last = first + keep_ref.shape[0]
         mass, _, total = joined(
-            keep[...], stat_ref[0:1, :], stat_ref[1:2, :], read_message(got, slice(None))
-        )
-        out_ref[:, part * half : (part + 1) * half] = (jnp.log(mass) - jnp.log(total)).T
+            keep_ref[...], stat_ref[0:1, :], stat_ref[1:2, :], read_message(message_ref, slice(None))
+        )
+        out_ref[:, first:last] = (jnp.log(mass) - jnp.log(total)).T
+        first = last
 
 
 def fits(queries, references, labels):
@@ -260,68 +272,72 @@
     )
 
 
+def spans(classes):
+    steps = [cut * classes // 512 for cut in CUTS]
+    return steps if all(cut % LANES == 0 for cut in steps) else [0, classes]
+
+
 def per_device(queries, references, labels):
     if not fits(queries, references, labels):
         return plain(queries, references, labels)
+    return exchanged(queries, references, labels)
+
+
+def exchanged(queries, references, labels):
     count, width = references.shape
     rows, classes = queries.shape[0], labels.shape[1]
-    half = classes // 2
+    cuts = spans(classes)
+    heights = [last - first for first, last in zip(cuts, cuts[1:])]
+    parts = len(heights)
     pair = 2 * LANES
     score_flops = 2 * count * rows * width
-    mass_flops = 4 * count * rows * half
+    mass_flops = [4 * count * rows * height for height in heights]
 
     far_refs = swapped(references, "blk", 2)
     mate_refs = swapped(references, "blk", 1)
     place = lax.axis_index("ref").astype(jnp.int32).reshape(1)
-    ordered, upper, lower = call(
-        arrange_kernel,
-        [((rows, width), BF16), ((half, count), BF16), ((half, count), BF16)],
+    ordered, *own_labels = call(
+        functools.partial(arrange_kernel, cuts),
+        [((rows, width), BF16)] + [((height, count), BF16) for height in heights],
         [SMEM, VMEM, VMEM],
         0,
-        "arrange",
     )(place, queries, labels)
-    far_labels = [swapped(part, "blk", 2) for part in (upper, lower)]
-    mate_labels = [swapped(part, "blk", 1) for part in (upper, lower)]
-    own_upper, own_lower, own_stat = call(
+    far_labels = [swapped(part, "blk", 2) for part in own_labels]
+    mate_labels = [swapped(part, "blk", 1) for part in own_labels]
+    *own_masses, own_stat = call(
         own_kernel,
-        [((half, rows), F32), ((half, rows), F32), ((8, rows), F32)],
-        [VMEM] * 7,
-        2 * score_flops + 2 * mass_flops,
-        "own",
-    )(ordered, references, mate_refs, upper, mate_labels[0], lower, mate_labels[1])
+        [((height, rows), F32) for height in heights] + [((8, rows), F32)],
+        [VMEM] * (3 + 2 * parts),
+        2 * score_flops + 2 * sum(mass_flops),
+    )(ordered, references, mate_refs, *own_labels, *mate_labels)
     cross_refs = swapped(far_refs, "blk", 1)
     cross_labels = [swapped(part, "blk", 1) for part in far_labels]
     (scores,) = call(
-        score_kernel, [((count, rows), F32)], [VMEM] * 2, score_flops, "score"
+        score_kernel, [((count, rows), F32)], [VMEM] * 2, score_flops
     )(ordered, far_refs)
     weights, stat = call(
-        weight_kernel,
-        [((2 * count, rows), BF16), ((8, rows), F32)],
-        [VMEM] * 4,
-        score_flops,
-        "weight",
+        weight_kernel, [((2 * count, rows), BF16), ((8, rows), F32)], [VMEM] * 4, score_flops
     )(ordered, cross_refs, scores, own_stat)
     got, kept = [], []
-    for own, far, cross in zip((own_upper, own_lower), far_labels, cross_labels):
+    for i in range(parts):
+        height = heights[i]
         message, keep = call(
             mass_kernel,
-            [((half + STAT_ROWS, pair), BF16), ((half, pair), F32)],
+            [((height + STAT_ROWS, pair), BF16), ((height, pair), F32)],
             [VMEM] * 5,
-            mass_flops,
-            "mass",
-        )(far, cross, weights, own, stat)
+            mass_flops[i],
+        )(far_labels[i], cross_labels[i], weights, own_masses[i], stat)
         received = swapped(message, "ref", 1)
         message, keep, near_stat = call(
             halve_kernel,
-            [((half + STAT_ROWS, LANES), BF16), ((half, LANES), F32), ((8, LANES), F32)],
+            [((height + STAT_ROWS, LANES), BF16), ((height, LANES), F32), ((8, LANES), F32)],
             [VMEM] * 3,
             0,
-            "halve",
         )(received, keep, stat)
         got.append(swapped(message, "ref", 2))
         kept.append(keep)
-    (out,) = call(final_kernel, [((LANES, classes), F32)], [VMEM] * 5, 0, "final")(
-        *got, *kept, near_stat
+    (out,) = call(final_kernel, [((LANES, classes), F32)], [VMEM] * (1 + 2 * parts), 0)(
+        near_stat, *got, *kept
     )
     return out
 

time: 46.6 us -> 46.5 us (level)
  waiting for transfers between devices: 25.1 us -> 26.4 us
  starting transfers between devices: 13.5 us -> 12.8 us
  local copies, waits for them, and re-layouts: 2.72 us -> 2.18 us
    ppermute x13, waiting for transfers between devices: 25.1 us -> 26.4 us  [swapped(): lax.ppermute(value, axis, [(i, i ^ bit) for i in range(lax.axis_size(axis...]
    ppermute x13, starting transfers between devices: 13.5 us -> 12.8 us  [swapped(): lax.ppermute(value, axis, [(i, i ^ bit) for i in range(lax.axis_size(axis...]
    unnamed x6, local copies, waits for them, and re-layouts: 2.72 us -> 2.18 us
where the time goes in v2:
time: 46.5 us; the launch traced here: 46.3 us
  waiting for transfers between devices  26.4 us (57%)
  starting transfers between devices  12.8 us (28%)
  Pallas kernels  4.92 us (11%)
  local copies, waits for them, and re-layouts  2.18 us (5%)
    ppermute x13, waiting for transfers between devices, swapped(): lax.ppermute(value, axis, [(i, i ^ bit) for i in range(lax.axis_size(axis...  26.4 us
    ppermute x13, starting transfers between devices, swapped(): lax.ppermute(value, axis, [(i, i ^ bit) for i in range(lax.axis_size(axis...  12.8 us
    unnamed x6, local copies, waits for them, and re-layouts  2.18 us
    pallas_call x1, Pallas kernels, exchanged(): call(own_kernel, [((height, rows), F32) for height in heights] + [((8, ro...  1.41 us
  transfers between devices with their start and end apart: 13, of which 6 were waited for; matrix products, arithmetic and copies ran while one was open for 0% of the time, Pallas kernels for 9%

profile of v2, /device:TPU:0, one launch (start us, length us, event | category | flops | bytes accessed | tf_op | source)
XLA Modules:
  0.0 46.3 jit_solution(13677090407587574264)
XLA Ops:
  0.0 3.0 %collective-permute-start.2 = (bf16[256,1024]{1,0:T(8,128)(2,1)}, bf16[256,1024]{1,0:T(8,128)(2,1)S(1)}, u32[]{:S(2)}, u32[]{:S(2)}) collective-permute-start(bf16[256,1024]{1,0:T(8,128)(2,1)} %refs_a.1), channel_id=1, source_target_pairs={{0,8},{4,12},{8,0},{12,4},{1,9},{5,13},{9,1},{13,5},{2,10},{6,14},... | collective-permute-start | bytes 1572872 | tf_op jit(solution)/shard_map/ppermute | solution.py:105
  3.0 12.1 %collective-permute-done.2.refs_ref = bf16[256,1024]{1,0:T(8,128)(2,1)S(1)} collective-permute-done((bf16[256,1024]{1,0:T(8,128)(2,1)}, bf16[256,1024]{1,0:T(8,128)(2,1)S(1)}, u32[]{:S(2)}, u32[]{:S(2)}) %collective-permute-start.2) | collective-permute-done | bytes 524320 | tf_op jit(solution)/shard_map/ppermute | solution.py:105
  15.1 1.2 %copy-done = bf16[512,1024]{1,0:T(8,128)(2,1)S(1)} copy-done((bf16[512,1024]{1,0:T(8,128)(2,1)S(1)}, bf16[512,1024]{1,0:T(8,128)(2,1)}, u32[]{:S(2)}) %copy-start) | copy-done | bytes 1048600
  16.4 0.9 %copy-done.1 = bf16[256,512]{1,0:T(8,128)(2,1)S(1)} copy-done((bf16[256,512]{1,0:T(8,128)(2,1)S(1)}, bf16[256,512]{1,0:T(8,128)(2,1)}, u32[]{:S(2)}) %copy-start.1) | copy-done | bytes 262168
  17.3 0.1 shard_map.37
  17.4 0.6 %collective-permute-start.5 = (bf16[256,256]{1,0:T(8,128)(2,1)S(1)}, bf16[256,256]{1,0:T(8,128)(2,1)S(1)}, u32[]{:S(2)}, u32[]{:S(2)}) collective-permute-start(bf16[256,256]{1,0:T(8,128)(2,1)S(1)} %get-tuple-element.24.refs_0_), channel_id=1, source_target_pairs={{0,4},{4,0},{8,12},{12,8},{1,5},{5,1},{9,13},{13,9},{2,6},{6,2},{1... | collective-permute-start | bytes 393224 | tf_op jit(solution)/shard_map/ppermute | solution.py:105
  18.0 1.7 %collective-permute-start.8 = (bf16[256,256]{1,0:T(8,128)(2,1)S(1)}, bf16[256,256]{1,0:T(8,128)(2,1)S(1)}, u32[]{:S(2)}, u32[]{:S(2)}) collective-permute-start(bf16[256,256]{1,0:T(8,128)(2,1)S(1)} %get-tuple-element.24.refs_0_), channel_id=1, source_target_pairs={{0,8},{4,12},{8,0},{12,4},{1,9},{5,13},{9,1},{13,5},{2,10},{6,14},... | collective-permute-start | bytes 393224 | tf_op jit(solution)/shard_map/ppermute | solution.py:105
  19.7 0.3 collective-permute-start
  20.0 4.3 %collective-permute-done.8.label_a = bf16[256,256]{1,0:T(8,128)(2,1)S(1)} collective-permute-done((bf16[256,256]{1,0:T(8,128)(2,1)S(1)}, bf16[256,256]{1,0:T(8,128)(2,1)S(1)}, u32[]{:S(2)}, u32[]{:S(2)}) %collective-permute-start.8) | collective-permute-done | bytes 131104 | tf_op jit(solution)/shard_map/ppermute | solution.py:105
  24.4 0.5 %shard_map.38.scores_ref = f32[256,512]{1,0:T(8,128)S(1)} custom-call(bf16[512,1024]{1,0:T(8,128)(2,1)S(1)} %get-tuple-element.23.queries_ref, bf16[256,1024]{1,0:T(8,128)(2,1)S(1)} %collective-permute-done.2.refs_ref), custom_call_target="tpu_custom_call" | custom-call | flops 268435456 | bytes 524288 | tf_op jit(solution)/shard_map/pallas_call | solution.py:315
  24.9 1.4 %collective-permute-done.label_a = bf16[256,256]{1,0:T(8,128)(2,1)S(1)} collective-permute-done((bf16[256,256]{1,0:T(8,128)(2,1)S(1)}, bf16[256,256]{1,0:T(8,128)(2,1)S(1)}, u32[]{:S(2)}, u32[]{:S(2)}) %collective-permute-start) | collective-permute-done | bytes 131104 | tf_op jit(solution)/shard_map/ppermute | solution.py:105
  26.3 1.4 %shard_map.39 = (f32[256,512]{1,0:T(8,128)S(1)}, f32[256,512]{1,0:T(8,128)S(1)}, f32[8,512]{1,0:T(8,128)S(1)}) custom-call(bf16[512,1024]{1,0:T(8,128)(2,1)S(1)} %get-tuple-element.23.queries_ref, bf16[256,1024]{1,0:T(8,128)(2,1)S(1)} %copy-done.2, bf16[256,1024]{1,0:T(8,128)(2,1)S(1)} %collective-permute-done.4.refs_b, ...), custom_call_target="tpu_custom_call" | custom-call | flops 1073741824 | bytes 1064960 | tf_op jit(solution)/shard_map/pallas_call | solution.py:307
  27.8 0.8 %shard_map.40 = (bf16[512,512]{1,0:T(8,128)(2,1)S(1)}, f32[8,512]{1,0:T(8,128)S(1)}) custom-call(bf16[512,1024]{1,0:T(8,128)(2,1)S(1)} %get-tuple-element.23.queries_ref, bf16[256,1024]{1,0:T(8,128)(2,1)S(1)} %collective-permute-done.3.refs_ref, f32[256,512]{1,0:T(8,128)S(1)} %shard_map.38.scores_ref, f32[8,512]{1,0:T(8,128)S(1)} %get-tuple-element.25.stat_ref), custom_call_target="tpu_custom_call" | custom-call | flops 268435456 | bytes 540672 | tf_op jit(solution)/shard_map/pallas_call | solution.py:318
  28.5 0.3 shard_map.43
  28.9 1.9 %collective-permute-start.10 = (bf16[272,256]{1,0:T(8,128)(2,1)S(1)}, bf16[272,256]{1,0:T(8,128)(2,1)S(1)}, u32[]{:S(2)}, u32[]{:S(2)}) collective-permute-start(bf16[272,256]{1,0:T(8,128)(2,1)S(1)} %get-tuple-element.33), channel_id=1, source_target_pairs={{0,1},{1,0},{2,3},{3,2},{4,5},{5,4},{6,7},{7,6},{8,9},{9,8},{10,11... | collective-permute-start | bytes 417800 | tf_op jit(solution)/shard_map/ppermute | solution.py:105
  30.7 0.3 shard_map.41
  31.0 0.3 collective-permute-start.7
  31.3 4.1 %collective-permute-done.10.received_ref = bf16[272,256]{1,0:T(8,128)(2,1)S(1)} collective-permute-done((bf16[272,256]{1,0:T(8,128)(2,1)S(1)}, bf16[272,256]{1,0:T(8,128)(2,1)S(1)}, u32[]{:S(2)}, u32[]{:S(2)}) %collective-permute-start.10) | collective-permute-done | bytes 139296 | tf_op jit(solution)/shard_map/ppermute | solution.py:105
  35.5 0.6 %shard_map.44 = (bf16[272,128]{1,0:T(8,128)(2,1)S(1)}, f32[256,128]{1,0:T(8,128)S(1)}, f32[8,128]{1,0:T(8,128)}) custom-call(bf16[272,256]{1,0:T(8,128)(2,1)S(1)} %collective-permute-done.10.received_ref, f32[256,256]{1,0:T(8,128)S(1)} %get-tuple-element.34.keep_ref, f32[8,512]{1,0:T(8,128)S(1)} %get-tuple-element.28.stat_ref), custom_call_target="tpu_custom_call" | custom-call | bytes 204800 | tf_op jit(solution)/shard_map/pallas_call | solution.py:331
  36.1 2.8 %collective-permute-start.11 = (bf16[272,128]{1,0:T(8,128)(2,1)S(1)}, bf16[272,128]{1,0:T(8,128)(2,1)S(1)}, u32[]{:S(2)}, u32[]{:S(2)}) collective-permute-start(bf16[272,128]{1,0:T(8,128)(2,1)S(1)} %get-tuple-element.35), channel_id=1, source_target_pairs={{0,2},{1,3},{2,0},{3,1},{4,6},{5,7},{6,4},{7,5},{8,10},{9,11},{10,... | collective-permute-start | bytes 208904 | tf_op jit(solution)/shard_map/ppermute | solution.py:105
  39.0 2.2 %collective-permute-start.12 = (bf16[272,128]{1,0:T(8,128)(2,1)S(1)}, bf16[272,128]{1,0:T(8,128)(2,1)S(1)}, u32[]{:S(2)}, u32[]{:S(2)}) collective-permute-start(bf16[272,128]{1,0:T(8,128)(2,1)S(1)} %get-tuple-element.36), channel_id=1, source_target_pairs={{0,2},{1,3},{2,0},{3,1},{4,6},{5,7},{6,4},{7,5},{8,10},{9,11},{10,... | collective-permute-start | bytes 208904 | tf_op jit(solution)/shard_map/ppermute | solution.py:105
  41.2 2.4 %collective-permute-done.11.refs_0_ = bf16[272,128]{1,0:T(8,128)(2,1)S(1)} collective-permute-done((bf16[272,128]{1,0:T(8,128)(2,1)S(1)}, bf16[272,128]{1,0:T(8,128)(2,1)S(1)}, u32[]{:S(2)}, u32[]{:S(2)}) %collective-permute-start.11) | collective-permute-done | bytes 69664 | tf_op jit(solution)/shard_map/ppermute | solution.py:105
  43.5 1.9 %collective-permute-done.12.refs_1_ = bf16[272,128]{1,0:T(8,128)(2,1)S(1)} collective-permute-done((bf16[272,128]{1,0:T(8,128)(2,1)S(1)}, bf16[272,128]{1,0:T(8,128)(2,1)S(1)}, u32[]{:S(2)}, u32[]{:S(2)}) %collective-permute-start.12) | collective-permute-done | bytes 69664 | tf_op jit(solution)/shard_map/ppermute | solution.py:105
  45.5 0.9 %shard_map.45 = f32[128,512]{1,0:T(8,128)} custom-call(f32[8,128]{1,0:T(8,128)S(1)} %get-tuple-element.31.stat_ref, bf16[272,128]{1,0:T(8,128)(2,1)S(1)} %collective-permute-done.11.refs_0_, bf16[272,128]{1,0:T(8,128)(2,1)S(1)} %collective-permute-done.12.refs_1_, f32[256,128]{1,0:T(8,128)S(1)} %get-tuple-element.37.refs_2_, ...), custom_call_target="tpu_custom_call" | custom-call | bytes 262144 | tf_op jit(solution)/shard_map/pallas_call | solution.py:339
  (17 shorter events, 0.1 us)
Async XLA Ops:
  0.0 15.1 %collective-permute-start.2 = (bf16[256,1024]{1,0:T(8,128)(2,1)}, bf16[256,1024]{1,0:T(8,128)(2,1)S(1)}, u32[]{:S(2)}, u32[]{:S(2)}) collective-permute-start(bf16[256,1024]{1,0:T(8,128)(2,1)} %refs_a.1), channel_id=1, source_target_pairs={{0,8},{4,12},{8,0},{12,4},{1,9},{5,13},{9,1},{13,5},{2,10},{6,14},... | collective-permute-start | bytes 1572872 | tf_op jit(solution)/shard_map/ppermute | solution.py:105
  3.0 23.3 %collective-permute-start.4 = (bf16[256,1024]{1,0:T(8,128)(2,1)}, bf16[256,1024]{1,0:T(8,128)(2,1)S(1)}, u32[]{:S(2)}, u32[]{:S(2)}) collective-permute-start(bf16[256,1024]{1,0:T(8,128)(2,1)} %refs_a.1), channel_id=1, source_target_pairs={{0,4},{4,0},{8,12},{12,8},{1,5},{5,1},{9,13},{13,9},{2,6},{6,2},{1... | collective-permute-start | bytes 1572872 | tf_op jit(solution)/shard_map/ppermute | solution.py:105
  15.1 12.6 %collective-permute-start.3 = (bf16[256,1024]{1,0:T(8,128)(2,1)S(1)}, bf16[256,1024]{1,0:T(8,128)(2,1)S(1)}, u32[]{:S(2)}, u32[]{:S(2)}) collective-permute-start(bf16[256,1024]{1,0:T(8,128)(2,1)S(1)} %collective-permute-done.2.refs_ref), channel_id=1, source_target_pairs={{0,4},{4,0},{8,12},{12,8},{1,5},{5,1},{9,13},{13,9},{2,6},{6,2},{1... | collective-permute-start | bytes 1572872 | tf_op jit(solution)/shard_map/ppermute | solution.py:105
  15.1 1.2 %copy-start = (bf16[512,1024]{1,0:T(8,128)(2,1)S(1)}, bf16[512,1024]{1,0:T(8,128)(2,1)}, u32[]{:S(2)}) copy-start(bf16[512,1024]{1,0:T(8,128)(2,1)} %queries_ref.1) | copy-start | bytes 3145732
  16.4 0.9 %copy-start.1 = (bf16[256,512]{1,0:T(8,128)(2,1)S(1)}, bf16[256,512]{1,0:T(8,128)(2,1)}, u32[]{:S(2)}) copy-start(bf16[256,512]{1,0:T(8,128)(2,1)} %labels_ref.1) | copy-start | bytes 786436
  17.4 2.6 %collective-permute-start.5 = (bf16[256,256]{1,0:T(8,128)(2,1)S(1)}, bf16[256,256]{1,0:T(8,128)(2,1)S(1)}, u32[]{:S(2)}, u32[]{:S(2)}) collective-permute-start(bf16[256,256]{1,0:T(8,128)(2,1)S(1)} %get-tuple-element.24.refs_0_), channel_id=1, source_target_pairs={{0,4},{4,0},{8,12},{12,8},{1,5},{5,1},{9,13},{13,9},{2,6},{6,2},{1... | collective-permute-start | bytes 393224 | tf_op jit(solution)/shard_map/ppermute | solution.py:105
  18.0 6.4 %collective-permute-start.8 = (bf16[256,256]{1,0:T(8,128)(2,1)S(1)}, bf16[256,256]{1,0:T(8,128)(2,1)S(1)}, u32[]{:S(2)}, u32[]{:S(2)}) collective-permute-start(bf16[256,256]{1,0:T(8,128)(2,1)S(1)} %get-tuple-element.24.refs_0_), channel_id=1, source_target_pairs={{0,8},{4,12},{8,0},{12,4},{1,9},{5,13},{9,1},{13,5},{2,10},{6,14},... | collective-permute-start | bytes 393224 | tf_op jit(solution)/shard_map/ppermute | solution.py:105
  19.7 6.5 %collective-permute-start = (bf16[256,256]{1,0:T(8,128)(2,1)S(1)}, bf16[256,256]{1,0:T(8,128)(2,1)S(1)}, u32[]{:S(2)}, u32[]{:S(2)}) collective-permute-start(bf16[256,256]{1,0:T(8,128)(2,1)S(1)} %get-tuple-element.22.refs_1_), channel_id=1, source_target_pairs={{0,8},{4,12},{8,0},{12,4},{1,9},{5,13},{9,1},{13,5},{2,10},{6,14},... | collective-permute-start | bytes 393224 | tf_op jit(solution)/shard_map/ppermute | solution.py:105
  20.0 6.3 %collective-permute-start.6 = (bf16[256,256]{1,0:T(8,128)(2,1)S(1)}, bf16[256,256]{1,0:T(8,128)(2,1)S(1)}, u32[]{:S(2)}, u32[]{:S(2)}) collective-permute-start(bf16[256,256]{1,0:T(8,128)(2,1)S(1)} %get-tuple-element.22.refs_1_), channel_id=1, source_target_pairs={{0,4},{4,0},{8,12},{12,8},{1,5},{5,1},{9,13},{13,9},{2,6},{6,2},{1... | collective-permute-start | bytes 393224 | tf_op jit(solution)/shard_map/ppermute | solution.py:105
  24.4 4.2 %collective-permute-start.9 = (bf16[256,256]{1,0:T(8,128)(2,1)S(1)}, bf16[256,256]{1,0:T(8,128)(2,1)S(1)}, u32[]{:S(2)}, u32[]{:S(2)}) collective-permute-start(bf16[256,256]{1,0:T(8,128)(2,1)S(1)} %collective-permute-done.8.label_a), channel_id=1, source_target_pairs={{0,4},{4,0},{8,12},{12,8},{1,5},{5,1},{9,13},{13,9},{2,6},{6,2},{1... | collective-permute-start | bytes 393224 | tf_op jit(solution)/shard_map/ppermute | solution.py:105
  24.4 1.9 %copy-start.2 = (bf16[256,1024]{1,0:T(8,128)(2,1)S(1)}, bf16[256,1024]{1,0:T(8,128)(2,1)}, u32[]{:S(2)}) copy-start(bf16[256,1024]{1,0:T(8,128)(2,1)} %refs_a.1) | copy-start | bytes 1572868
  26.3 4.4 %collective-permute-start.1 = (bf16[256,256]{1,0:T(8,128)(2,1)S(1)}, bf16[256,256]{1,0:T(8,128)(2,1)S(1)}, u32[]{:S(2)}, u32[]{:S(2)}) collective-permute-start(bf16[256,256]{1,0:T(8,128)(2,1)S(1)} %collective-permute-done.label_a), channel_id=1, source_target_pairs={{0,4},{4,0},{8,12},{12,8},{1,5},{5,1},{9,13},{13,9},{2,6},{6,2},{1... | collective-permute-start | bytes 393224 | tf_op jit(solution)/shard_map/ppermute | solution.py:105
  28.9 6.6 %collective-permute-start.10 = (bf16[272,256]{1,0:T(8,128)(2,1)S(1)}, bf16[272,256]{1,0:T(8,128)(2,1)S(1)}, u32[]{:S(2)}, u32[]{:S(2)}) collective-permute-start(bf16[272,256]{1,0:T(8,128)(2,1)S(1)} %get-tuple-element.33), channel_id=1, source_target_pairs={{0,1},{1,0},{2,3},{3,2},{4,5},{5,4},{6,7},{7,6},{8,9},{9,8},{10,11... | collective-permute-start | bytes 417800 | tf_op jit(solution)/shard_map/ppermute | solution.py:105
  31.0 7.9 %collective-permute-start.7 = (bf16[272,256]{1,0:T(8,128)(2,1)S(1)}, bf16[272,256]{1,0:T(8,128)(2,1)S(1)}, u32[]{:S(2)}, u32[]{:S(2)}) collective-permute-start(bf16[272,256]{1,0:T(8,128)(2,1)S(1)} %get-tuple-element.29), channel_id=1, source_target_pairs={{0,1},{1,0},{2,3},{3,2},{4,5},{5,4},{6,7},{7,6},{8,9},{9,8},{10,11... | collective-permute-start | bytes 417800 | tf_op jit(solution)/shard_map/ppermute | solution.py:105
  36.1 7.4 %collective-permute-start.11 = (bf16[272,128]{1,0:T(8,128)(2,1)S(1)}, bf16[272,128]{1,0:T(8,128)(2,1)S(1)}, u32[]{:S(2)}, u32[]{:S(2)}) collective-permute-start(bf16[272,128]{1,0:T(8,128)(2,1)S(1)} %get-tuple-element.35), channel_id=1, source_target_pairs={{0,2},{1,3},{2,0},{3,1},{4,6},{5,7},{6,4},{7,5},{8,10},{9,11},{10,... | collective-permute-start | bytes 208904 | tf_op jit(solution)/shard_map/ppermute | solution.py:105
  39.0 6.5 %collective-permute-start.12 = (bf16[272,128]{1,0:T(8,128)(2,1)S(1)}, bf16[272,128]{1,0:T(8,128)(2,1)S(1)}, u32[]{:S(2)}, u32[]{:S(2)}) collective-permute-start(bf16[272,128]{1,0:T(8,128)(2,1)S(1)} %get-tuple-element.36), channel_id=1, source_target_pairs={{0,2},{1,3},{2,0},{3,1},{4,6},{5,7},{6,4},{7,5},{8,10},{9,11},{10,... | collective-permute-start | bytes 208904 | tf_op jit(solution)/shard_map/ppermute | solution.py:105

commit v3 on v2

--- a/solution.py
+++ b/solution.py
@@ -157,68 +157,68 @@
     stat_ref[1:2, :] = total
 
 
-def score_kernel(queries_ref, refs_ref, scores_ref):
-    scores_ref[...] = scored(refs_ref[...], queries_ref[...])
-
-
-def weight_kernel(queries_ref, refs_ref, scores_ref, stat_ref, weights_ref, out_ref):
-    scores_a = scores_ref[...]
-    scores_b = scored(refs_ref[...], queries_ref[...])
-    rows = scores_a.shape[0]
-    top = jnp.maximum(
-        jnp.max(scores_a, axis=0, keepdims=True), jnp.max(scores_b, axis=0, keepdims=True)
-    )
-    own_top = stat_ref[0:1, :]
-    top = jnp.maximum(even_top(top), own_top)
-    weights_a = jnp.exp(scores_a - top).astype(BF16)
-    weights_b = jnp.exp(scores_b - top).astype(BF16)
-    weights_ref[:rows, :] = weights_a
-    weights_ref[rows:, :] = weights_b
-    shrink = jnp.exp(own_top - top)
-    total = (
-        stat_ref[1:2, :] * shrink
-        + jnp.sum(weights_a.astype(F32), axis=0, keepdims=True)
-        + jnp.sum(weights_b.astype(F32), axis=0, keepdims=True)
-    )
+def far_kernel(queries_ref, refs_ref, stat_ref, weights_ref, out_ref):
+    scores = scored(refs_ref[...], queries_ref[...])
+    old_top = stat_ref[0:1, :]
+    top = jnp.maximum(even_top(jnp.max(scores, axis=0, keepdims=True)), old_top)
+    weights = jnp.exp(scores - top).astype(BF16)
+    weights_ref[...] = weights
+    shrink = jnp.exp(old_top - top)
+    total = stat_ref[1:2, :] * shrink + jnp.sum(weights.astype(F32), axis=0, keepdims=True)
     out_ref[0:1, :] = top
     out_ref[1:2, :] = total
     out_ref[2:3, :] = shrink
 
 
-def write_message(message_ref, columns, mass, top, total):
-    height = mass.shape[0]
+def write_stats(message_ref, height, top, total):
     high = total.astype(BF16)
     low = (total - high.astype(F32)).astype(BF16)
-    message_ref[:height, columns] = mass.astype(BF16)
-    row = lax.broadcasted_iota(jnp.int32, (STAT_ROWS, mass.shape[1]), 0)
-    stats = jnp.where(
-        row == 0, top, jnp.where(row == 1, high.astype(F32), low.astype(F32))
-    )
-    message_ref[height:, columns] = stats.astype(BF16)
-
-
-def read_message(message_ref, columns):
+    row = lax.broadcasted_iota(jnp.int32, (STAT_ROWS, total.shape[1]), 0)
+    stats = jnp.where(row == 0, top, jnp.where(row == 1, high.astype(F32), low.astype(F32)))
+    message_ref[height:, :] = stats.astype(BF16)
+
+
+def write_message(message_ref, mass, top, total):
+    height = mass.shape[0]
+    message_ref[:height, :] = mass.astype(BF16)
+    write_stats(message_ref, height, top, total)
+
+
+def read_message(message_ref, first=0, last=None):
     height = message_ref.shape[0] - STAT_ROWS
-    mass = message_ref[:height, columns].astype(F32)
-    stats = message_ref[height:, columns].astype(F32)
+    mass = message_ref[first : last or height, :].astype(F32)
+    stats = message_ref[height:, :].astype(F32)
     return mass, stats[0:1], stats[1:2] + stats[2:3]
 
 
-def mass_kernel(label_a, label_b, weights_ref, own_ref, stat_ref, message_ref, keep_ref):
-    rows = label_a.shape[1]
-    mass = (
-        own_ref[...] * stat_ref[2:3, :]
-        + jnp.dot(label_a[...], weights_ref[:rows, :], preferred_element_type=F32)
-        + jnp.dot(label_b[...], weights_ref[rows:, :], preferred_element_type=F32)
-    )
-    for slot in range(2):
-        columns = slice(slot * LANES, (slot + 1) * LANES)
-        kept = slice(2 * slot * LANES, (2 * slot + 1) * LANES)
-        sent = slice((2 * slot + 1) * LANES, (2 * slot + 2) * LANES)
-        write_message(
-            message_ref, columns, mass[:, sent], stat_ref[0:1, sent], stat_ref[1:2, sent]
-        )
-        keep_ref[:, columns] = mass[:, kept]
+def cross_mass(far_labels, cross_labels, far_weights, cross_weights, own_ref, far_stat, stat_ref):
+    mass = own_ref[...] * far_stat[2:3, :] + jnp.dot(
+        far_labels[...], far_weights[...], preferred_element_type=F32
+    )
+    return mass * stat_ref[2:3, :] + jnp.dot(
+        cross_labels[...], cross_weights[...], preferred_element_type=F32
+    )
+
+
+def block_of(index):
+    return slice(index * LANES, (index + 1) * LANES)
+
+
+def mass_kernel(*refs):
+    stat_ref, earlier, (far_ref, near_ref, middle_ref, keep_ref) = refs[6], refs[7:-4], refs[-4:]
+    mass = cross_mass(*refs[:7])
+    sent = block_of(3)
+    write_message(far_ref, mass[:, sent], stat_ref[0:1, sent], stat_ref[1:2, sent])
+    middle_ref[...] = mass[:, block_of(2)]
+    keep_ref[...] = mass[:, block_of(0)]
+    first = 0
+    for piece_ref in earlier:
+        near_ref[: piece_ref.shape[0], :] = piece_ref[...]
+        first = piece_ref.shape[0]
+    last = first + mass.shape[0]
+    near_ref[first:last, :] = mass[:, block_of(1)].astype(BF16)
+    if near_ref.shape[0] > last:
+        write_stats(near_ref, last, stat_ref[0:1, block_of(1)], stat_ref[1:2, block_of(1)])
 
 
 def joined(mass, top, total, other):
@@ -233,32 +233,39 @@
     )
 
 
-def halve_kernel(received_ref, keep_ref, stat_ref, message_ref, out_ref, out_stat_ref):
-    near, far = slice(0, LANES), slice(LANES, 2 * LANES)
-    block = slice(2 * LANES, 3 * LANES)
-    mass, top, total = joined(
-        keep_ref[:, far], stat_ref[0:1, block], stat_ref[1:2, block], read_message(received_ref, far)
-    )
-    write_message(message_ref, slice(None), mass, top, total)
-    mass, top, total = joined(
-        keep_ref[:, near], stat_ref[0:1, near], stat_ref[1:2, near], read_message(received_ref, near)
-    )
-    out_ref[...] = mass
+def halve_kernel(received_ref, middle_ref, stat_ref, message_ref):
+    block = block_of(2)
+    write_message(
+        message_ref,
+        *joined(
+            middle_ref[...],
+            stat_ref[0:1, block],
+            stat_ref[1:2, block],
+            read_message(received_ref),
+        ),
+    )
+
+
+def logged(mass, top, total):
+    return (jnp.log(mass) - jnp.log(total)).T
+
+
+def early_kernel(near_ref, last_ref, keep_a, keep_b, stat_ref, out_ref, mass_ref, out_stat_ref):
+    top, total = stat_ref[0:1, block_of(0)], stat_ref[1:2, block_of(0)]
+    cut = keep_a.shape[0]
+    part = joined(keep_a[...], top, total, read_message(near_ref, 0, cut))
+    out_ref[...] = logged(*joined(*part, read_message(last_ref)))
+    mass, top, total = joined(keep_b[...], top, total, read_message(near_ref, cut))
+    mass_ref[...] = mass
     out_stat_ref[0:1, :] = top
     out_stat_ref[1:2, :] = total
 
 
-def final_kernel(stat_ref, *refs):
-    parts = len(refs) // 2
-    got, kept, out_ref = refs[:parts], refs[parts : 2 * parts], refs[-1]
-    first = 0
-    for message_ref, keep_ref in zip(got, kept):
-        last = first + keep_ref.shape[0]
-        mass, _, total = joined(
-            keep_ref[...], stat_ref[0:1, :], stat_ref[1:2, :], read_message(message_ref, slice(None))
-        )
-        out_ref[:, first:last] = (jnp.log(mass) - jnp.log(total)).T
-        first = last
+def final_kernel(early_ref, last_ref, mass_ref, stat_ref, out_ref):
+    early = early_ref.shape[1]
+    out_ref[:, :early] = early_ref[...]
+    part = mass_ref[...], stat_ref[0:1, :], stat_ref[1:2, :]
+    out_ref[:, early:] = logged(*joined(*part, read_message(last_ref)))
 
 
 def fits(queries, references, labels):
@@ -289,7 +296,6 @@
     cuts = spans(classes)
     heights = [last - first for first, last in zip(cuts, cuts[1:])]
     parts = len(heights)
-    pair = 2 * LANES
     score_flops = 2 * count * rows * width
     mass_flops = [4 * count * rows * height for height in heights]
 
@@ -312,32 +318,54 @@
     )(ordered, references, mate_refs, *own_labels, *mate_labels)
     cross_refs = swapped(far_refs, "blk", 1)
     cross_labels = [swapped(part, "blk", 1) for part in far_labels]
-    (scores,) = call(
-        score_kernel, [((count, rows), F32)], [VMEM] * 2, score_flops
-    )(ordered, far_refs)
-    weights, stat = call(
-        weight_kernel, [((2 * count, rows), BF16), ((8, rows), F32)], [VMEM] * 4, score_flops
-    )(ordered, cross_refs, scores, own_stat)
-    got, kept = [], []
-    for i in range(parts):
-        height = heights[i]
-        message, keep = call(
-            mass_kernel,
-            [((height + STAT_ROWS, pair), BF16), ((height, pair), F32)],
-            [VMEM] * 5,
-            mass_flops[i],
-        )(far_labels[i], cross_labels[i], weights, own_masses[i], stat)
-        received = swapped(message, "ref", 1)
-        message, keep, near_stat = call(
-            halve_kernel,
-            [((height + STAT_ROWS, LANES), BF16), ((height, LANES), F32), ((8, LANES), F32)],
-            [VMEM] * 3,
-            0,
-        )(received, keep, stat)
-        got.append(swapped(message, "ref", 2))
+    stat_shape = ((8, rows), F32)
+    far_weights, far_stat = call(
+        far_kernel, [((count, rows), BF16), stat_shape], [VMEM] * 3, score_flops
+    )(ordered, far_refs, own_stat)
+    cross_weights, stat = call(
+        far_kernel, [((count, rows), BF16), stat_shape], [VMEM] * 3, score_flops
+    )(ordered, cross_refs, far_stat)
+
+    def operands(i):
+        return (
+            far_labels[i],
+            cross_labels[i],
+            far_weights,
+            cross_weights,
+            own_masses[i],
+            far_stat,
+            stat,
+        )
+
+    def message_shape(height):
+        return ((height + STAT_ROWS, LANES), BF16)
+
+    near, kept, lasts = (), [], []
+    for i, height in enumerate(heights):
+        sizes = [
+            message_shape(height),
+            message_shape(classes) if i else ((height, LANES), BF16),
+            ((height, LANES), F32),
+            ((height, LANES), F32),
+        ]
+        far, piece, middle, keep = call(
+            mass_kernel, sizes, [VMEM] * (7 + len(near)), mass_flops[i]
+        )(*operands(i), *near)
+        near = (piece,)
         kept.append(keep)
-    (out,) = call(final_kernel, [((LANES, classes), F32)], [VMEM] * (1 + 2 * parts), 0)(
-        near_stat, *got, *kept
+        (message,) = call(halve_kernel, [message_shape(height)], [VMEM] * 3, 0)(
+            swapped(far, "ref", 1), middle, stat
+        )
+        lasts.append(swapped(message, "ref", 2))
+    near = swapped(*near, "ref", 1)
+    early, mass, near_stat = call(
+        early_kernel,
+        [((LANES, heights[0]), F32), ((heights[1], LANES), F32), ((8, LANES), F32)],
+        [VMEM] * 5,
+        0,
+    )(near, lasts[0], *kept, stat)
+    (out,) = call(final_kernel, [((LANES, classes), F32)], [VMEM] * 4, 0)(
+        early, lasts[1], mass, near_stat
     )
     return out
 

time: 46.5 us -> 45.5 us (0.978)
  waiting for transfers between devices: 26.4 us -> 23.8 us
  starting transfers between devices: 12.8 us -> 14.8 us
  Pallas kernels: 4.92 us -> 4.45 us
    ppermute x13 -> x14, waiting for transfers between devices: 26.4 us -> 23.8 us  [swapped(): lax.ppermute(value, axis, [(i, i ^ bit) for i in range(lax.axis_size(axis...]
    ppermute x13 -> x14, starting transfers between devices: 12.8 us -> 14.8 us  [swapped(): lax.ppermute(value, axis, [(i, i ^ bit) for i in range(lax.axis_size(axis...]
    pallas_call x7 -> x8, Pallas kernels: 3.38 us -> 2.92 us  [the longest x2 1.26 us: exchanged(): call(far_kernel, [((count, rows), BF16), stat_shape], [VMEM] * 3, score_f...]
  transfers between devices with their start and end apart: 13 -> 14, of which waited for: 6 -> 6; matrix products, arithmetic and copies ran while one was open for 0% -> 0% of each run, Pallas kernels for 9% -> 8%
where the time goes in v3:
time: 45.5 us; the launch traced here: 45.3 us
  waiting for transfers between devices  23.8 us (52%)
  starting transfers between devices  14.8 us (33%)
  Pallas kernels  4.45 us (10%)
  local copies, waits for them, and re-layouts  2.18 us (5%)
    ppermute x14, waiting for transfers between devices, swapped(): lax.ppermute(value, axis, [(i, i ^ bit) for i in range(lax.axis_size(axis...  23.8 us
    ppermute x14, starting transfers between devices, swapped(): lax.ppermute(value, axis, [(i, i ^ bit) for i in range(lax.axis_size(axis...  14.8 us
    unnamed x6, local copies, waits for them, and re-layouts  2.18 us
    pallas_call x1, Pallas kernels, exchanged(): call(own_kernel, [((height, rows), F32) for height in heights] + [((8, ro...  1.42 us
    pallas_call x2, Pallas kernels, exchanged(): call(far_kernel, [((count, rows), BF16), stat_shape], [VMEM] * 3, score_f...  1.26 us
  transfers between devices with their start and end apart: 14, of which 6 were waited for; matrix products, arithmetic and copies ran while one was open for 0% of the time, Pallas kernels for 8%

profile of v3, /device:TPU:0, one launch (start us, length us, event | category | flops | bytes accessed | tf_op | source)
XLA Modules:
  0.0 45.3 jit_solution(9755986879044953782)
XLA Ops:
  0.0 3.0 %collective-permute-start.2 = (bf16[256,1024]{1,0:T(8,128)(2,1)}, bf16[256,1024]{1,0:T(8,128)(2,1)S(1)}, u32[]{:S(2)}, u32[]{:S(2)}) collective-permute-start(bf16[256,1024]{1,0:T(8,128)(2,1)} %refs_a.1), channel_id=1, source_target_pairs={{0,8},{4,12},{8,0},{12,4},{1,9},{5,13},{9,1},{13,5},{2,10},{6,14},... | collective-permute-start | bytes 1572872 | tf_op jit(solution)/shard_map/ppermute | solution.py:105
  3.0 12.1 %collective-permute-done.2.refs_ref = bf16[256,1024]{1,0:T(8,128)(2,1)S(1)} collective-permute-done((bf16[256,1024]{1,0:T(8,128)(2,1)}, bf16[256,1024]{1,0:T(8,128)(2,1)S(1)}, u32[]{:S(2)}, u32[]{:S(2)}) %collective-permute-start.2) | collective-permute-done | bytes 524320 | tf_op jit(solution)/shard_map/ppermute | solution.py:105
  15.1 1.2 %copy-done = bf16[512,1024]{1,0:T(8,128)(2,1)S(1)} copy-done((bf16[512,1024]{1,0:T(8,128)(2,1)S(1)}, bf16[512,1024]{1,0:T(8,128)(2,1)}, u32[]{:S(2)}) %copy-start) | copy-done | bytes 1048600
  16.4 0.9 %copy-done.1 = bf16[256,512]{1,0:T(8,128)(2,1)S(1)} copy-done((bf16[256,512]{1,0:T(8,128)(2,1)S(1)}, bf16[256,512]{1,0:T(8,128)(2,1)}, u32[]{:S(2)}) %copy-start.1) | copy-done | bytes 262168
  17.4 0.6 %collective-permute-start.4 = (bf16[256,256]{1,0:T(8,128)(2,1)S(1)}, bf16[256,256]{1,0:T(8,128)(2,1)S(1)}, u32[]{:S(2)}, u32[]{:S(2)}) collective-permute-start(bf16[256,256]{1,0:T(8,128)(2,1)S(1)} %get-tuple-element.28.refs_0_), channel_id=1, source_target_pairs={{0,4},{4,0},{8,12},{12,8},{1,5},{5,1},{9,13},{13,9},{2,6},{6,2},{1... | collective-permute-start | bytes 393224 | tf_op jit(solution)/shard_map/ppermute | solution.py:105
  18.0 1.7 %collective-permute-start.7 = (bf16[256,256]{1,0:T(8,128)(2,1)S(1)}, bf16[256,256]{1,0:T(8,128)(2,1)S(1)}, u32[]{:S(2)}, u32[]{:S(2)}) collective-permute-start(bf16[256,256]{1,0:T(8,128)(2,1)S(1)} %get-tuple-element.28.refs_0_), channel_id=1, source_target_pairs={{0,8},{4,12},{8,0},{12,4},{1,9},{5,13},{9,1},{13,5},{2,10},{6,14},... | collective-permute-start | bytes 393224 | tf_op jit(solution)/shard_map/ppermute | solution.py:105
  19.7 0.3 collective-permute-start
  20.0 4.3 %collective-permute-done.7.refs_0_ = bf16[256,256]{1,0:T(8,128)(2,1)S(1)} collective-permute-done((bf16[256,256]{1,0:T(8,128)(2,1)S(1)}, bf16[256,256]{1,0:T(8,128)(2,1)S(1)}, u32[]{:S(2)}, u32[]{:S(2)}) %collective-permute-start.7) | collective-permute-done | bytes 131104 | tf_op jit(solution)/shard_map/ppermute | solution.py:105
  24.4 1.9 %collective-permute-done.refs_0_ = bf16[256,256]{1,0:T(8,128)(2,1)S(1)} collective-permute-done((bf16[256,256]{1,0:T(8,128)(2,1)S(1)}, bf16[256,256]{1,0:T(8,128)(2,1)S(1)}, u32[]{:S(2)}, u32[]{:S(2)}) %collective-permute-start) | collective-permute-done | bytes 131104 | tf_op jit(solution)/shard_map/ppermute | solution.py:105
  26.3 1.4 %shard_map.38 = (f32[256,512]{1,0:T(8,128)S(1)}, f32[256,512]{1,0:T(8,128)S(1)}, f32[8,512]{1,0:T(8,128)S(1)}) custom-call(bf16[512,1024]{1,0:T(8,128)(2,1)S(1)} %get-tuple-element.27.queries_ref, bf16[256,1024]{1,0:T(8,128)(2,1)S(1)} %copy-done.2, bf16[256,1024]{1,0:T(8,128)(2,1)S(1)} %collective-permute-done.3.refs_b, ...), custom_call_target="tpu_custom_call" | custom-call | flops 1073741824 | bytes 1064960 | tf_op jit(solution)/shard_map/pallas_call | solution.py:313
  27.7 0.6 %shard_map.39 = (bf16[256,512]{1,0:T(8,128)(2,1)S(1)}, f32[8,512]{1,0:T(8,128)S(1)}) custom-call(bf16[512,1024]{1,0:T(8,128)(2,1)S(1)} %get-tuple-element.27.queries_ref, bf16[256,1024]{1,0:T(8,128)(2,1)S(1)} %collective-permute-done.2.refs_ref, f32[8,512]{1,0:T(8,128)S(1)} %get-tuple-element.29.stat_ref), custom_call_target="tpu_custom_call" | custom-call | flops 268435456 | bytes 278528 | tf_op jit(solution)/shard_map/pallas_call | solution.py:322
  28.4 0.6 %shard_map.40 = (bf16[256,512]{1,0:T(8,128)(2,1)S(1)}, f32[8,512]{1,0:T(8,128)S(1)}) custom-call(bf16[512,1024]{1,0:T(8,128)(2,1)S(1)} %get-tuple-element.27.queries_ref, bf16[256,1024]{1,0:T(8,128)(2,1)S(1)} %collective-permute-done.6.refs_ref, f32[8,512]{1,0:T(8,128)S(1)} %get-tuple-element.31.stat_ref.refs_5_), custom_call_target="tpu_custom_call" | custom-call | flops 268435456 | bytes 278528 | tf_op jit(solution)/shard_map/pallas_call | solution.py:325
  29.0 0.3 shard_map.41
  29.3 1.9 %collective-permute-start.10 = (bf16[272,128]{1,0:T(8,128)(2,1)S(1)}, bf16[272,128]{1,0:T(8,128)(2,1)S(1)}, u32[]{:S(2)}, u32[]{:S(2)}) collective-permute-start(bf16[272,128]{1,0:T(8,128)(2,1)S(1)} %get-tuple-element.38), channel_id=1, source_target_pairs={{0,1},{1,0},{2,3},{3,2},{4,5},{5,4},{6,7},{7,6},{8,9},{9,8},{10,11... | collective-permute-start | bytes 208904 | tf_op jit(solution)/shard_map/ppermute | solution.py:105
  31.2 0.3 shard_map.42
  31.5 0.3 collective-permute-start.12
  31.8 1.8 %collective-permute-start.9 = (bf16[528,128]{1,0:T(8,128)(2,1)S(1)}, bf16[528,128]{1,0:T(8,128)(2,1)S(1)}, u32[]{:S(2)}, u32[]{:S(2)}) collective-permute-start(bf16[528,128]{1,0:T(8,128)(2,1)S(1)} %get-tuple-element.37), channel_id=1, source_target_pairs={{0,1},{1,0},{2,3},{3,2},{4,5},{5,4},{6,7},{7,6},{8,9},{9,8},{10,11... | collective-permute-start | bytes 405512 | tf_op jit(solution)/shard_map/ppermute | solution.py:105
  33.6 0.4 collective-permute-done.10.received_ref
  34.1 2.8 %collective-permute-start.11 = (bf16[272,128]{1,0:T(8,128)(2,1)S(1)}, bf16[272,128]{1,0:T(8,128)(2,1)S(1)}, u32[]{:S(2)}, u32[]{:S(2)}) collective-permute-start(bf16[272,128]{1,0:T(8,128)(2,1)S(1)} %shard_map.43), channel_id=1, source_target_pairs={{0,2},{1,3},{2,0},{3,1},{4,6},{5,7},{6,4},{7,5},{8,10},{9,11},{10,... | collective-permute-start | bytes 208904 | tf_op jit(solution)/shard_map/ppermute | solution.py:105
  36.9 2.4 %collective-permute-start.13 = (bf16[272,128]{1,0:T(8,128)(2,1)S(1)}, bf16[272,128]{1,0:T(8,128)(2,1)S(1)}, u32[]{:S(2)}, u32[]{:S(2)}) collective-permute-start(bf16[272,128]{1,0:T(8,128)(2,1)S(1)} %shard_map.45), channel_id=1, source_target_pairs={{0,2},{1,3},{2,0},{3,1},{4,6},{5,7},{6,4},{7,5},{8,10},{9,11},{10,... | collective-permute-start | bytes 208904 | tf_op jit(solution)/shard_map/ppermute | solution.py:105
  39.3 1.5 %collective-permute-done.9.near_ref = bf16[528,128]{1,0:T(8,128)(2,1)S(1)} collective-permute-done((bf16[528,128]{1,0:T(8,128)(2,1)S(1)}, bf16[528,128]{1,0:T(8,128)(2,1)S(1)}, u32[]{:S(2)}, u32[]{:S(2)}) %collective-permute-start.9) | collective-permute-done | bytes 135200 | tf_op jit(solution)/shard_map/ppermute | solution.py:105
  40.8 0.2 shard_map.44
  41.0 3.5 %collective-permute-done.13.last_ref = bf16[272,128]{1,0:T(8,128)(2,1)S(1)} collective-permute-done((bf16[272,128]{1,0:T(8,128)(2,1)S(1)}, bf16[272,128]{1,0:T(8,128)(2,1)S(1)}, u32[]{:S(2)}, u32[]{:S(2)}) %collective-permute-start.13) | collective-permute-done | bytes 69664 | tf_op jit(solution)/shard_map/ppermute | solution.py:105
  44.5 0.8 %shard_map.46 = f32[128,512]{1,0:T(8,128)} custom-call(f32[128,256]{1,0:T(8,128)S(1)} %get-tuple-element.42.early_ref, bf16[272,128]{1,0:T(8,128)(2,1)S(1)} %collective-permute-done.13.last_ref, f32[256,128]{1,0:T(8,128)S(1)} %get-tuple-element.45.mass_ref, f32[8,128]{1,0:T(8,128)S(1)} %get-tuple-element.46.stat_ref), custom_call_target="tpu_custom_call" | custom-call | bytes 262144 | tf_op jit(solution)/shard_map/pallas_call | solution.py:367
  (20 shorter events, 0.2 us)
Async XLA Ops:
  0.0 15.1 %collective-permute-start.2 = (bf16[256,1024]{1,0:T(8,128)(2,1)}, bf16[256,1024]{1,0:T(8,128)(2,1)S(1)}, u32[]{:S(2)}, u32[]{:S(2)}) collective-permute-start(bf16[256,1024]{1,0:T(8,128)(2,1)} %refs_a.1), channel_id=1, source_target_pairs={{0,8},{4,12},{8,0},{12,4},{1,9},{5,13},{9,1},{13,5},{2,10},{6,14},... | collective-permute-start | bytes 1572872 | tf_op jit(solution)/shard_map/ppermute | solution.py:105
  3.0 23.3 %collective-permute-start.3 = (bf16[256,1024]{1,0:T(8,128)(2,1)}, bf16[256,1024]{1,0:T(8,128)(2,1)S(1)}, u32[]{:S(2)}, u32[]{:S(2)}) collective-permute-start(bf16[256,1024]{1,0:T(8,128)(2,1)} %refs_a.1), channel_id=1, source_target_pairs={{0,4},{4,0},{8,12},{12,8},{1,5},{5,1},{9,13},{13,9},{2,6},{6,2},{1... | collective-permute-start | bytes 1572872 | tf_op jit(solution)/shard_map/ppermute | solution.py:105
  15.1 13.3 %collective-permute-start.6 = (bf16[256,1024]{1,0:T(8,128)(2,1)S(1)}, bf16[256,1024]{1,0:T(8,128)(2,1)S(1)}, u32[]{:S(2)}, u32[]{:S(2)}) collective-permute-start(bf16[256,1024]{1,0:T(8,128)(2,1)S(1)} %collective-permute-done.2.refs_ref), channel_id=1, source_target_pairs={{0,4},{4,0},{8,12},{12,8},{1,5},{5,1},{9,13},{13,9},{2,6},{6,2},{1... | collective-permute-start | bytes 1572872 | tf_op jit(solution)/shard_map/ppermute | solution.py:105
  15.1 1.2 %copy-start = (bf16[512,1024]{1,0:T(8,128)(2,1)S(1)}, bf16[512,1024]{1,0:T(8,128)(2,1)}, u32[]{:S(2)}) copy-start(bf16[512,1024]{1,0:T(8,128)(2,1)} %queries_ref.1) | copy-start | bytes 3145732
  16.4 0.9 %copy-start.1 = (bf16[256,512]{1,0:T(8,128)(2,1)S(1)}, bf16[256,512]{1,0:T(8,128)(2,1)}, u32[]{:S(2)}) copy-start(bf16[256,512]{1,0:T(8,128)(2,1)} %labels_ref.1) | copy-start | bytes 786436
  17.3 9.0 %copy-start.2 = (bf16[256,1024]{1,0:T(8,128)(2,1)S(1)}, bf16[256,1024]{1,0:T(8,128)(2,1)}, u32[]{:S(2)}) copy-start(bf16[256,1024]{1,0:T(8,128)(2,1)} %refs_a.1) | copy-start | bytes 1572868
  17.4 2.6 %collective-permute-start.4 = (bf16[256,256]{1,0:T(8,128)(2,1)S(1)}, bf16[256,256]{1,0:T(8,128)(2,1)S(1)}, u32[]{:S(2)}, u32[]{:S(2)}) collective-permute-start(bf16[256,256]{1,0:T(8,128)(2,1)S(1)} %get-tuple-element.28.refs_0_), channel_id=1, source_target_pairs={{0,4},{4,0},{8,12},{12,8},{1,5},{5,1},{9,13},{13,9},{2,6},{6,2},{1... | collective-permute-start | bytes 393224 | tf_op jit(solution)/shard_map/ppermute | solution.py:105
  18.0 6.4 %collective-permute-start.7 = (bf16[256,256]{1,0:T(8,128)(2,1)S(1)}, bf16[256,256]{1,0:T(8,128)(2,1)S(1)}, u32[]{:S(2)}, u32[]{:S(2)}) collective-permute-start(bf16[256,256]{1,0:T(8,128)(2,1)S(1)} %get-tuple-element.28.refs_0_), channel_id=1, source_target_pairs={{0,8},{4,12},{8,0},{12,4},{1,9},{5,13},{9,1},{13,5},{2,10},{6,14},... | collective-permute-start | bytes 393224 | tf_op jit(solution)/shard_map/ppermute | solution.py:105
  19.7 6.5 %collective-permute-start = (bf16[256,256]{1,0:T(8,128)(2,1)S(1)}, bf16[256,256]{1,0:T(8,128)(2,1)S(1)}, u32[]{:S(2)}, u32[]{:S(2)}) collective-permute-start(bf16[256,256]{1,0:T(8,128)(2,1)S(1)} %get-tuple-element.26.refs_1_), channel_id=1, source_target_pairs={{0,8},{4,12},{8,0},{12,4},{1,9},{5,13},{9,1},{13,5},{2,10},{6,14},... | collective-permute-start | bytes 393224 | tf_op jit(solution)/shard_map/ppermute | solution.py:105
  20.0 6.3 %collective-permute-start.5 = (bf16[256,256]{1,0:T(8,128)(2,1)S(1)}, bf16[256,256]{1,0:T(8,128)(2,1)S(1)}, u32[]{:S(2)}, u32[]{:S(2)}) collective-permute-start(bf16[256,256]{1,0:T(8,128)(2,1)S(1)} %get-tuple-element.26.refs_1_), channel_id=1, source_target_pairs={{0,4},{4,0},{8,12},{12,8},{1,5},{5,1},{9,13},{13,9},{2,6},{6,2},{1... | collective-permute-start | bytes 393224 | tf_op jit(solution)/shard_map/ppermute | solution.py:105
  24.4 4.6 %collective-permute-start.8 = (bf16[256,256]{1,0:T(8,128)(2,1)S(1)}, bf16[256,256]{1,0:T(8,128)(2,1)S(1)}, u32[]{:S(2)}, u32[]{:S(2)}) collective-permute-start(bf16[256,256]{1,0:T(8,128)(2,1)S(1)} %collective-permute-done.7.refs_0_), channel_id=1, source_target_pairs={{0,4},{4,0},{8,12},{12,8},{1,5},{5,1},{9,13},{13,9},{2,6},{6,2},{1... | collective-permute-start | bytes 393224 | tf_op jit(solution)/shard_map/ppermute | solution.py:105
  26.3 4.9 %collective-permute-start.1 = (bf16[256,256]{1,0:T(8,128)(2,1)S(1)}, bf16[256,256]{1,0:T(8,128)(2,1)S(1)}, u32[]{:S(2)}, u32[]{:S(2)}) collective-permute-start(bf16[256,256]{1,0:T(8,128)(2,1)S(1)} %collective-permute-done.refs_0_), channel_id=1, source_target_pairs={{0,4},{4,0},{8,12},{12,8},{1,5},{5,1},{9,13},{13,9},{2,6},{6,2},{1... | collective-permute-start | bytes 393224 | tf_op jit(solution)/shard_map/ppermute | solution.py:105
  29.3 4.7 %collective-permute-start.10 = (bf16[272,128]{1,0:T(8,128)(2,1)S(1)}, bf16[272,128]{1,0:T(8,128)(2,1)S(1)}, u32[]{:S(2)}, u32[]{:S(2)}) collective-permute-start(bf16[272,128]{1,0:T(8,128)(2,1)S(1)} %get-tuple-element.38), channel_id=1, source_target_pairs={{0,1},{1,0},{2,3},{3,2},{4,5},{5,4},{6,7},{7,6},{8,9},{9,8},{10,11... | collective-permute-start | bytes 208904 | tf_op jit(solution)/shard_map/ppermute | solution.py:105
  31.5 5.4 %collective-permute-start.12 = (bf16[272,128]{1,0:T(8,128)(2,1)S(1)}, bf16[272,128]{1,0:T(8,128)(2,1)S(1)}, u32[]{:S(2)}, u32[]{:S(2)}) collective-permute-start(bf16[272,128]{1,0:T(8,128)(2,1)S(1)} %get-tuple-element.43), channel_id=1, source_target_pairs={{0,1},{1,0},{2,3},{3,2},{4,5},{5,4},{6,7},{7,6},{8,9},{9,8},{10,11... | collective-permute-start | bytes 208904 | tf_op jit(solution)/shard_map/ppermute | solution.py:105
  31.8 9.0 %collective-permute-start.9 = (bf16[528,128]{1,0:T(8,128)(2,1)S(1)}, bf16[528,128]{1,0:T(8,128)(2,1)S(1)}, u32[]{:S(2)}, u32[]{:S(2)}) collective-permute-start(bf16[528,128]{1,0:T(8,128)(2,1)S(1)} %get-tuple-element.37), channel_id=1, source_target_pairs={{0,1},{1,0},{2,3},{3,2},{4,5},{5,4},{6,7},{7,6},{8,9},{9,8},{10,11... | collective-permute-start | bytes 405512 | tf_op jit(solution)/shard_map/ppermute | solution.py:105
  34.1 6.8 %collective-permute-start.11 = (bf16[272,128]{1,0:T(8,128)(2,1)S(1)}, bf16[272,128]{1,0:T(8,128)(2,1)S(1)}, u32[]{:S(2)}, u32[]{:S(2)}) collective-permute-start(bf16[272,128]{1,0:T(8,128)(2,1)S(1)} %shard_map.43), channel_id=1, source_target_pairs={{0,2},{1,3},{2,0},{3,1},{4,6},{5,7},{6,4},{7,5},{8,10},{9,11},{10,... | collective-permute-start | bytes 208904 | tf_op jit(solution)/shard_map/ppermute | solution.py:105
  36.9 7.5 %collective-permute-start.13 = (bf16[272,128]{1,0:T(8,128)(2,1)S(1)}, bf16[272,128]{1,0:T(8,128)(2,1)S(1)}, u32[]{:S(2)}, u32[]{:S(2)}) collective-permute-start(bf16[272,128]{1,0:T(8,128)(2,1)S(1)} %shard_map.45), channel_id=1, source_target_pairs={{0,2},{1,3},{2,0},{3,1},{4,6},{5,7},{6,4},{7,5},{8,10},{9,11},{10,... | collective-permute-start | bytes 208904 | tf_op jit(solution)/shard_map/ppermute | solution.py:105

commit v4 on v3

--- a/solution.py
+++ b/solution.py
@@ -170,25 +170,32 @@
     out_ref[2:3, :] = shrink
 
 
-def write_stats(message_ref, height, top, total):
-    high = total.astype(BF16)
-    low = (total - high.astype(F32)).astype(BF16)
-    row = lax.broadcasted_iota(jnp.int32, (STAT_ROWS, total.shape[1]), 0)
-    stats = jnp.where(row == 0, top, jnp.where(row == 1, high.astype(F32), low.astype(F32)))
-    message_ref[height:, :] = stats.astype(BF16)
+def halves_of(value):
+    high = value.astype(BF16).astype(F32)
+    return high, (value - high).astype(BF16).astype(F32)
+
+
+def center_of(mass):
+    least = jnp.min(mass, axis=0, keepdims=True)
+    return halves_of(jnp.minimum(jnp.mean(mass, axis=0, keepdims=True), 2.0 * least))
 
 
 def write_message(message_ref, mass, top, total):
     height = mass.shape[0]
-    message_ref[:height, :] = mass.astype(BF16)
-    write_stats(message_ref, height, top, total)
-
-
-def read_message(message_ref, first=0, last=None):
-    height = message_ref.shape[0] - STAT_ROWS
-    mass = message_ref[first : last or height, :].astype(F32)
-    stats = message_ref[height:, :].astype(F32)
-    return mass, stats[0:1], stats[1:2] + stats[2:3]
+    rows = (top, *halves_of(total), *center_of(mass))
+    message_ref[:height, :] = (mass - (rows[3] + rows[4])).astype(BF16)
+    index = lax.broadcasted_iota(jnp.int32, (STAT_ROWS, mass.shape[1]), 0)
+    stats = rows[-1]
+    for row in range(len(rows) - 1):
+        stats = jnp.where(index == row, rows[row], stats)
+    message_ref[height:, :] = stats.astype(BF16)
+
+
+def read_message(message_ref, first=0, last=None, row=3):
+    stats = message_ref[message_ref.shape[0] - STAT_ROWS :, :].astype(F32)
+    mass = message_ref[first : last or message_ref.shape[0] - STAT_ROWS, :].astype(F32)
+    center = stats[row : row + 1] + stats[row + 1 : row + 2]
+    return mass + center, stats[0:1], stats[1:2] + stats[2:3]
 
 
 def cross_mass(far_labels, cross_labels, far_weights, cross_weights, own_ref, far_stat, stat_ref):
@@ -207,18 +214,21 @@
 def mass_kernel(*refs):
     stat_ref, earlier, (far_ref, near_ref, middle_ref, keep_ref) = refs[6], refs[7:-4], refs[-4:]
     mass = cross_mass(*refs[:7])
-    sent = block_of(3)
+    sent, near = block_of(3), block_of(1)
     write_message(far_ref, mass[:, sent], stat_ref[0:1, sent], stat_ref[1:2, sent])
     middle_ref[...] = mass[:, block_of(2)]
     keep_ref[...] = mass[:, block_of(0)]
-    first = 0
+    if not earlier:
+        write_message(near_ref, mass[:, near], stat_ref[0:1, near], stat_ref[1:2, near])
     for piece_ref in earlier:
-        near_ref[: piece_ref.shape[0], :] = piece_ref[...]
-        first = piece_ref.shape[0]
-    last = first + mass.shape[0]
-    near_ref[first:last, :] = mass[:, block_of(1)].astype(BF16)
-    if near_ref.shape[0] > last:
-        write_stats(near_ref, last, stat_ref[0:1, block_of(1)], stat_ref[1:2, block_of(1)])
+        first = piece_ref.shape[0] - STAT_ROWS
+        last = first + mass.shape[0]
+        high, low = center_of(mass[:, near])
+        near_ref[:first, :] = piece_ref[:first, :]
+        near_ref[first:last, :] = (mass[:, near] - (high + low)).astype(BF16)
+        index = lax.broadcasted_iota(jnp.int32, (STAT_ROWS, LANES), 0)
+        stats = jnp.where(index == 5, high, jnp.where(index > 5, low, piece_ref[first:, :].astype(F32)))
+        near_ref[last:, :] = stats.astype(BF16)
 
 
 def joined(mass, top, total, other):
@@ -255,7 +265,7 @@
     cut = keep_a.shape[0]
     part = joined(keep_a[...], top, total, read_message(near_ref, 0, cut))
     out_ref[...] = logged(*joined(*part, read_message(last_ref)))
-    mass, top, total = joined(keep_b[...], top, total, read_message(near_ref, cut))
+    mass, top, total = joined(keep_b[...], top, total, read_message(near_ref, cut, None, 5))
     mass_ref[...] = mass
     out_stat_ref[0:1, :] = top
     out_stat_ref[1:2, :] = total
@@ -344,7 +354,7 @@
     for i, height in enumerate(heights):
         sizes = [
             message_shape(height),
-            message_shape(classes) if i else ((height, LANES), BF16),
+            message_shape(classes if i else height),
             ((height, LANES), F32),
             ((height, LANES), F32),
         ]

time: 45.5 us -> 45.6 us (level)
  no operation moved by 1% of the time
where the time goes in v4:
time: 45.6 us; the launch traced here: 45.4 us
  waiting for transfers between devices  23.8 us (52%)
  starting transfers between devices  14.8 us (32%)
  Pallas kernels  4.6 us (10%)
  local copies, waits for them, and re-layouts  2.18 us (5%)
    ppermute x14, waiting for transfers between devices, swapped(): lax.ppermute(value, axis, [(i, i ^ bit) for i in range(lax.axis_size(axis...  23.8 us
    ppermute x14, starting transfers between devices, swapped(): lax.ppermute(value, axis, [(i, i ^ bit) for i in range(lax.axis_size(axis...  14.8 us
    unnamed x6, local copies, waits for them, and re-layouts  2.18 us
    pallas_call x1, Pallas kernels, exchanged(): call(own_kernel, [((height, rows), F32) for height in heights] + [((8, ro...  1.42 us
    pallas_call x2, Pallas kernels, exchanged(): call(far_kernel, [((count, rows), BF16), stat_shape], [VMEM] * 3, score_f...  1.26 us
  transfers between devices with their start and end apart: 14, of which 6 were waited for; matrix products, arithmetic and copies ran while one was open for 0% of the time, Pallas kernels for 8%

profile of v4, /device:TPU:0, one launch (start us, length us, event | category | flops | bytes accessed | tf_op | source)
XLA Modules:
  0.0 45.4 jit_solution(11703081392528944253)
XLA Ops:
  0.0 3.0 %collective-permute-start.2 = (bf16[256,1024]{1,0:T(8,128)(2,1)}, bf16[256,1024]{1,0:T(8,128)(2,1)S(1)}, u32[]{:S(2)}, u32[]{:S(2)}) collective-permute-start(bf16[256,1024]{1,0:T(8,128)(2,1)} %refs_a.1), channel_id=1, source_target_pairs={{0,8},{4,12},{8,0},{12,4},{1,9},{5,13},{9,1},{13,5},{2,10},{6,14},... | collective-permute-start | bytes 1572872 | tf_op jit(solution)/shard_map/ppermute | solution.py:105
  3.0 12.1 %collective-permute-done.2.refs_ref = bf16[256,1024]{1,0:T(8,128)(2,1)S(1)} collective-permute-done((bf16[256,1024]{1,0:T(8,128)(2,1)}, bf16[256,1024]{1,0:T(8,128)(2,1)S(1)}, u32[]{:S(2)}, u32[]{:S(2)}) %collective-permute-start.2) | collective-permute-done | bytes 524320 | tf_op jit(solution)/shard_map/ppermute | solution.py:105
  15.1 1.2 %copy-done = bf16[512,1024]{1,0:T(8,128)(2,1)S(1)} copy-done((bf16[512,1024]{1,0:T(8,128)(2,1)S(1)}, bf16[512,1024]{1,0:T(8,128)(2,1)}, u32[]{:S(2)}) %copy-start) | copy-done | bytes 1048600
  16.4 0.9 %copy-done.1 = bf16[256,512]{1,0:T(8,128)(2,1)S(1)} copy-done((bf16[256,512]{1,0:T(8,128)(2,1)S(1)}, bf16[256,512]{1,0:T(8,128)(2,1)}, u32[]{:S(2)}) %copy-start.1) | copy-done | bytes 262168
  17.4 0.6 %collective-permute-start.4 = (bf16[256,256]{1,0:T(8,128)(2,1)S(1)}, bf16[256,256]{1,0:T(8,128)(2,1)S(1)}, u32[]{:S(2)}, u32[]{:S(2)}) collective-permute-start(bf16[256,256]{1,0:T(8,128)(2,1)S(1)} %get-tuple-element.28.refs_0_), channel_id=1, source_target_pairs={{0,4},{4,0},{8,12},{12,8},{1,5},{5,1},{9,13},{13,9},{2,6},{6,2},{1... | collective-permute-start | bytes 393224 | tf_op jit(solution)/shard_map/ppermute | solution.py:105
  18.0 1.7 %collective-permute-start.7 = (bf16[256,256]{1,0:T(8,128)(2,1)S(1)}, bf16[256,256]{1,0:T(8,128)(2,1)S(1)}, u32[]{:S(2)}, u32[]{:S(2)}) collective-permute-start(bf16[256,256]{1,0:T(8,128)(2,1)S(1)} %get-tuple-element.28.refs_0_), channel_id=1, source_target_pairs={{0,8},{4,12},{8,0},{12,4},{1,9},{5,13},{9,1},{13,5},{2,10},{6,14},... | collective-permute-start | bytes 393224 | tf_op jit(solution)/shard_map/ppermute | solution.py:105
  19.7 0.3 collective-permute-start
  20.0 4.3 %collective-permute-done.7.refs_0_ = bf16[256,256]{1,0:T(8,128)(2,1)S(1)} collective-permute-done((bf16[256,256]{1,0:T(8,128)(2,1)S(1)}, bf16[256,256]{1,0:T(8,128)(2,1)S(1)}, u32[]{:S(2)}, u32[]{:S(2)}) %collective-permute-start.7) | collective-permute-done | bytes 131104 | tf_op jit(solution)/shard_map/ppermute | solution.py:105
  24.4 1.9 %collective-permute-done.refs_0_ = bf16[256,256]{1,0:T(8,128)(2,1)S(1)} collective-permute-done((bf16[256,256]{1,0:T(8,128)(2,1)S(1)}, bf16[256,256]{1,0:T(8,128)(2,1)S(1)}, u32[]{:S(2)}, u32[]{:S(2)}) %collective-permute-start) | collective-permute-done | bytes 131104 | tf_op jit(solution)/shard_map/ppermute | solution.py:105
  26.3 1.4 %shard_map.38 = (f32[256,512]{1,0:T(8,128)S(1)}, f32[256,512]{1,0:T(8,128)S(1)}, f32[8,512]{1,0:T(8,128)S(1)}) custom-call(bf16[512,1024]{1,0:T(8,128)(2,1)S(1)} %get-tuple-element.27.queries_ref, bf16[256,1024]{1,0:T(8,128)(2,1)S(1)} %copy-done.2, bf16[256,1024]{1,0:T(8,128)(2,1)S(1)} %collective-permute-done.3.refs_b, ...), custom_call_target="tpu_custom_call" | custom-call | flops 1073741824 | bytes 1064960 | tf_op jit(solution)/shard_map/pallas_call | solution.py:323
  27.7 0.6 %shard_map.39 = (bf16[256,512]{1,0:T(8,128)(2,1)S(1)}, f32[8,512]{1,0:T(8,128)S(1)}) custom-call(bf16[512,1024]{1,0:T(8,128)(2,1)S(1)} %get-tuple-element.27.queries_ref, bf16[256,1024]{1,0:T(8,128)(2,1)S(1)} %collective-permute-done.2.refs_ref, f32[8,512]{1,0:T(8,128)S(1)} %get-tuple-element.29.stat_ref), custom_call_target="tpu_custom_call" | custom-call | flops 268435456 | bytes 278528 | tf_op jit(solution)/shard_map/pallas_call | solution.py:332
  28.4 0.6 %shard_map.40 = (bf16[256,512]{1,0:T(8,128)(2,1)S(1)}, f32[8,512]{1,0:T(8,128)S(1)}) custom-call(bf16[512,1024]{1,0:T(8,128)(2,1)S(1)} %get-tuple-element.27.queries_ref, bf16[256,1024]{1,0:T(8,128)(2,1)S(1)} %collective-permute-done.6.refs_ref, f32[8,512]{1,0:T(8,128)S(1)} %get-tuple-element.31.stat_ref.refs_5_), custom_call_target="tpu_custom_call" | custom-call | flops 268435456 | bytes 278528 | tf_op jit(solution)/shard_map/pallas_call | solution.py:335
  29.0 0.3 shard_map.41
  29.4 1.9 %collective-permute-start.10 = (bf16[272,128]{1,0:T(8,128)(2,1)S(1)}, bf16[272,128]{1,0:T(8,128)(2,1)S(1)}, u32[]{:S(2)}, u32[]{:S(2)}) collective-permute-start(bf16[272,128]{1,0:T(8,128)(2,1)S(1)} %get-tuple-element.38), channel_id=1, source_target_pairs={{0,1},{1,0},{2,3},{3,2},{4,5},{5,4},{6,7},{7,6},{8,9},{9,8},{10,11... | collective-permute-start | bytes 208904 | tf_op jit(solution)/shard_map/ppermute | solution.py:105
  31.2 0.3 shard_map.42
  31.6 0.3 collective-permute-start.12
  31.9 1.8 %collective-permute-start.9 = (bf16[528,128]{1,0:T(8,128)(2,1)S(1)}, bf16[528,128]{1,0:T(8,128)(2,1)S(1)}, u32[]{:S(2)}, u32[]{:S(2)}) collective-permute-start(bf16[528,128]{1,0:T(8,128)(2,1)S(1)} %get-tuple-element.37), channel_id=1, source_target_pairs={{0,1},{1,0},{2,3},{3,2},{4,5},{5,4},{6,7},{7,6},{8,9},{9,8},{10,11... | collective-permute-start | bytes 405512 | tf_op jit(solution)/shard_map/ppermute | solution.py:105
  33.7 0.4 collective-permute-done.10.received_ref
  34.1 2.8 %collective-permute-start.11 = (bf16[272,128]{1,0:T(8,128)(2,1)S(1)}, bf16[272,128]{1,0:T(8,128)(2,1)S(1)}, u32[]{:S(2)}, u32[]{:S(2)}) collective-permute-start(bf16[272,128]{1,0:T(8,128)(2,1)S(1)} %shard_map.43), channel_id=1, source_target_pairs={{0,2},{1,3},{2,0},{3,1},{4,6},{5,7},{6,4},{7,5},{8,10},{9,11},{10,... | collective-permute-start | bytes 208904 | tf_op jit(solution)/shard_map/ppermute | solution.py:105
  37.0 2.4 %collective-permute-start.13 = (bf16[272,128]{1,0:T(8,128)(2,1)S(1)}, bf16[272,128]{1,0:T(8,128)(2,1)S(1)}, u32[]{:S(2)}, u32[]{:S(2)}) collective-permute-start(bf16[272,128]{1,0:T(8,128)(2,1)S(1)} %shard_map.45), channel_id=1, source_target_pairs={{0,2},{1,3},{2,0},{3,1},{4,6},{5,7},{6,4},{7,5},{8,10},{9,11},{10,... | collective-permute-start | bytes 208904 | tf_op jit(solution)/shard_map/ppermute | solution.py:105
  39.4 1.4 %collective-permute-done.9.near_ref = bf16[528,128]{1,0:T(8,128)(2,1)S(1)} collective-permute-done((bf16[528,128]{1,0:T(8,128)(2,1)S(1)}, bf16[528,128]{1,0:T(8,128)(2,1)S(1)}, u32[]{:S(2)}, u32[]{:S(2)}) %collective-permute-start.9) | collective-permute-done | bytes 135200 | tf_op jit(solution)/shard_map/ppermute | solution.py:105
  40.8 0.2 shard_map.44
  41.0 3.6 %collective-permute-done.13.last_ref = bf16[272,128]{1,0:T(8,128)(2,1)S(1)} collective-permute-done((bf16[272,128]{1,0:T(8,128)(2,1)S(1)}, bf16[272,128]{1,0:T(8,128)(2,1)S(1)}, u32[]{:S(2)}, u32[]{:S(2)}) %collective-permute-start.13) | collective-permute-done | bytes 69664 | tf_op jit(solution)/shard_map/ppermute | solution.py:105
  44.6 0.8 %shard_map.46 = f32[128,512]{1,0:T(8,128)} custom-call(f32[128,256]{1,0:T(8,128)S(1)} %get-tuple-element.42.early_ref, bf16[272,128]{1,0:T(8,128)(2,1)S(1)} %collective-permute-done.13.last_ref, f32[256,128]{1,0:T(8,128)S(1)} %get-tuple-element.45.mass_ref, f32[8,128]{1,0:T(8,128)S(1)} %get-tuple-element.46.stat_ref), custom_call_target="tpu_custom_call" | custom-call | bytes 262144 | tf_op jit(solution)/shard_map/pallas_call | solution.py:377
  (20 shorter events, 0.3 us)
Async XLA Ops:
  0.0 15.1 %collective-permute-start.2 = (bf16[256,1024]{1,0:T(8,128)(2,1)}, bf16[256,1024]{1,0:T(8,128)(2,1)S(1)}, u32[]{:S(2)}, u32[]{:S(2)}) collective-permute-start(bf16[256,1024]{1,0:T(8,128)(2,1)} %refs_a.1), channel_id=1, source_target_pairs={{0,8},{4,12},{8,0},{12,4},{1,9},{5,13},{9,1},{13,5},{2,10},{6,14},... | collective-permute-start | bytes 1572872 | tf_op jit(solution)/shard_map/ppermute | solution.py:105
  3.0 23.3 %collective-permute-start.3 = (bf16[256,1024]{1,0:T(8,128)(2,1)}, bf16[256,1024]{1,0:T(8,128)(2,1)S(1)}, u32[]{:S(2)}, u32[]{:S(2)}) collective-permute-start(bf16[256,1024]{1,0:T(8,128)(2,1)} %refs_a.1), channel_id=1, source_target_pairs={{0,4},{4,0},{8,12},{12,8},{1,5},{5,1},{9,13},{13,9},{2,6},{6,2},{1... | collective-permute-start | bytes 1572872 | tf_op jit(solution)/shard_map/ppermute | solution.py:105
  15.1 13.3 %collective-permute-start.6 = (bf16[256,1024]{1,0:T(8,128)(2,1)S(1)}, bf16[256,1024]{1,0:T(8,128)(2,1)S(1)}, u32[]{:S(2)}, u32[]{:S(2)}) collective-permute-start(bf16[256,1024]{1,0:T(8,128)(2,1)S(1)} %collective-permute-done.2.refs_ref), channel_id=1, source_target_pairs={{0,4},{4,0},{8,12},{12,8},{1,5},{5,1},{9,13},{13,9},{2,6},{6,2},{1... | collective-permute-start | bytes 1572872 | tf_op jit(solution)/shard_map/ppermute | solution.py:105
  15.1 1.2 %copy-start = (bf16[512,1024]{1,0:T(8,128)(2,1)S(1)}, bf16[512,1024]{1,0:T(8,128)(2,1)}, u32[]{:S(2)}) copy-start(bf16[512,1024]{1,0:T(8,128)(2,1)} %queries_ref.1) | copy-start | bytes 3145732
  16.4 0.9 %copy-start.1 = (bf16[256,512]{1,0:T(8,128)(2,1)S(1)}, bf16[256,512]{1,0:T(8,128)(2,1)}, u32[]{:S(2)}) copy-start(bf16[256,512]{1,0:T(8,128)(2,1)} %labels_ref.1) | copy-start | bytes 786436
  17.3 9.0 %copy-start.2 = (bf16[256,1024]{1,0:T(8,128)(2,1)S(1)}, bf16[256,1024]{1,0:T(8,128)(2,1)}, u32[]{:S(2)}) copy-start(bf16[256,1024]{1,0:T(8,128)(2,1)} %refs_a.1) | copy-start | bytes 1572868
  17.4 2.6 %collective-permute-start.4 = (bf16[256,256]{1,0:T(8,128)(2,1)S(1)}, bf16[256,256]{1,0:T(8,128)(2,1)S(1)}, u32[]{:S(2)}, u32[]{:S(2)}) collective-permute-start(bf16[256,256]{1,0:T(8,128)(2,1)S(1)} %get-tuple-element.28.refs_0_), channel_id=1, source_target_pairs={{0,4},{4,0},{8,12},{12,8},{1,5},{5,1},{9,13},{13,9},{2,6},{6,2},{1... | collective-permute-start | bytes 393224 | tf_op jit(solution)/shard_map/ppermute | solution.py:105
  18.0 6.4 %collective-permute-start.7 = (bf16[256,256]{1,0:T(8,128)(2,1)S(1)}, bf16[256,256]{1,0:T(8,128)(2,1)S(1)}, u32[]{:S(2)}, u32[]{:S(2)}) collective-permute-start(bf16[256,256]{1,0:T(8,128)(2,1)S(1)} %get-tuple-element.28.refs_0_), channel_id=1, source_target_pairs={{0,8},{4,12},{8,0},{12,4},{1,9},{5,13},{9,1},{13,5},{2,10},{6,14},... | collective-permute-start | bytes 393224 | tf_op jit(solution)/shard_map/ppermute | solution.py:105
  19.7 6.5 %collective-permute-start = (bf16[256,256]{1,0:T(8,128)(2,1)S(1)}, bf16[256,256]{1,0:T(8,128)(2,1)S(1)}, u32[]{:S(2)}, u32[]{:S(2)}) collective-permute-start(bf16[256,256]{1,0:T(8,128)(2,1)S(1)} %get-tuple-element.26.refs_1_), channel_id=1, source_target_pairs={{0,8},{4,12},{8,0},{12,4},{1,9},{5,13},{9,1},{13,5},{2,10},{6,14},... | collective-permute-start | bytes 393224 | tf_op jit(solution)/shard_map/ppermute | solution.py:105
  20.0 6.3 %collective-permute-start.5 = (bf16[256,256]{1,0:T(8,128)(2,1)S(1)}, bf16[256,256]{1,0:T(8,128)(2,1)S(1)}, u32[]{:S(2)}, u32[]{:S(2)}) collective-permute-start(bf16[256,256]{1,0:T(8,128)(2,1)S(1)} %get-tuple-element.26.refs_1_), channel_id=1, source_target_pairs={{0,4},{4,0},{8,12},{12,8},{1,5},{5,1},{9,13},{13,9},{2,6},{6,2},{1... | collective-permute-start | bytes 393224 | tf_op jit(solution)/shard_map/ppermute | solution.py:105
  24.4 4.6 %collective-permute-start.8 = (bf16[256,256]{1,0:T(8,128)(2,1)S(1)}, bf16[256,256]{1,0:T(8,128)(2,1)S(1)}, u32[]{:S(2)}, u32[]{:S(2)}) collective-permute-start(bf16[256,256]{1,0:T(8,128)(2,1)S(1)} %collective-permute-done.7.refs_0_), channel_id=1, source_target_pairs={{0,4},{4,0},{8,12},{12,8},{1,5},{5,1},{9,13},{13,9},{2,6},{6,2},{1... | collective-permute-start | bytes 393224 | tf_op jit(solution)/shard_map/ppermute | solution.py:105
  26.3 4.9 %collective-permute-start.1 = (bf16[256,256]{1,0:T(8,128)(2,1)S(1)}, bf16[256,256]{1,0:T(8,128)(2,1)S(1)}, u32[]{:S(2)}, u32[]{:S(2)}) collective-permute-start(bf16[256,256]{1,0:T(8,128)(2,1)S(1)} %collective-permute-done.refs_0_), channel_id=1, source_target_pairs={{0,4},{4,0},{8,12},{12,8},{1,5},{5,1},{9,13},{13,9},{2,6},{6,2},{1... | collective-permute-start | bytes 393224 | tf_op jit(solution)/shard_map/ppermute | solution.py:105
  29.4 4.7 %collective-permute-start.10 = (bf16[272,128]{1,0:T(8,128)(2,1)S(1)}, bf16[272,128]{1,0:T(8,128)(2,1)S(1)}, u32[]{:S(2)}, u32[]{:S(2)}) collective-permute-start(bf16[272,128]{1,0:T(8,128)(2,1)S(1)} %get-tuple-element.38), channel_id=1, source_target_pairs={{0,1},{1,0},{2,3},{3,2},{4,5},{5,4},{6,7},{7,6},{8,9},{9,8},{10,11... | collective-permute-start | bytes 208904 | tf_op jit(solution)/shard_map/ppermute | solution.py:105
  31.6 5.4 %collective-permute-start.12 = (bf16[272,128]{1,0:T(8,128)(2,1)S(1)}, bf16[272,128]{1,0:T(8,128)(2,1)S(1)}, u32[]{:S(2)}, u32[]{:S(2)}) collective-permute-start(bf16[272,128]{1,0:T(8,128)(2,1)S(1)} %get-tuple-element.43), channel_id=1, source_target_pairs={{0,1},{1,0},{2,3},{3,2},{4,5},{5,4},{6,7},{7,6},{8,9},{9,8},{10,11... | collective-permute-start | bytes 208904 | tf_op jit(solution)/shard_map/ppermute | solution.py:105
  31.9 9.0 %collective-permute-start.9 = (bf16[528,128]{1,0:T(8,128)(2,1)S(1)}, bf16[528,128]{1,0:T(8,128)(2,1)S(1)}, u32[]{:S(2)}, u32[]{:S(2)}) collective-permute-start(bf16[528,128]{1,0:T(8,128)(2,1)S(1)} %get-tuple-element.37), channel_id=1, source_target_pairs={{0,1},{1,0},{2,3},{3,2},{4,5},{5,4},{6,7},{7,6},{8,9},{9,8},{10,11... | collective-permute-start | bytes 405512 | tf_op jit(solution)/shard_map/ppermute | solution.py:105
  34.1 6.7 %collective-permute-start.11 = (bf16[272,128]{1,0:T(8,128)(2,1)S(1)}, bf16[272,128]{1,0:T(8,128)(2,1)S(1)}, u32[]{:S(2)}, u32[]{:S(2)}) collective-permute-start(bf16[272,128]{1,0:T(8,128)(2,1)S(1)} %shard_map.43), channel_id=1, source_target_pairs={{0,2},{1,3},{2,0},{3,1},{4,6},{5,7},{6,4},{7,5},{8,10},{9,11},{10,... | collective-permute-start | bytes 208904 | tf_op jit(solution)/shard_map/ppermute | solution.py:105
  37.0 7.5 %collective-permute-start.13 = (bf16[272,128]{1,0:T(8,128)(2,1)S(1)}, bf16[272,128]{1,0:T(8,128)(2,1)S(1)}, u32[]{:S(2)}, u32[]{:S(2)}) collective-permute-start(bf16[272,128]{1,0:T(8,128)(2,1)S(1)} %shard_map.45), channel_id=1, source_target_pairs={{0,2},{1,3},{2,0},{3,1},{4,6},{5,7},{6,4},{7,5},{8,10},{9,11},{10,... | collective-permute-start | bytes 208904 | tf_op jit(solution)/shard_map/ppermute | solution.py:105

commit v5 on v4

--- a/solution.py
+++ b/solution.py
@@ -88,14 +88,15 @@
 SMEM = pl.BlockSpec(memory_space=pltpu.SMEM)
 
 
-def call(kernel, outs, in_specs, flops):
+def call(kernel, outs, in_specs, flops, out_space=VMEM, scratch=()):
     shapes = [jax.ShapeDtypeStruct(shape, dtype) for shape, dtype in outs]
     moved = sum(math.prod(shape) * jnp.dtype(dtype).itemsize for shape, dtype in outs)
     return pl.pallas_call(
         kernel,
         out_shape=shapes,
         in_specs=in_specs,
-        out_specs=[VMEM] * len(shapes),
+        out_specs=[out_space] * len(shapes),
+        scratch_shapes=scratch,
         cost_estimate=pl.CostEstimate(flops=flops, bytes_accessed=moved, transcendentals=0),
         compiler_params=pltpu.CompilerParams(vmem_limit_bytes=GRANT),
     )
@@ -271,11 +272,16 @@
     out_stat_ref[1:2, :] = total
 
 
-def final_kernel(early_ref, last_ref, mass_ref, stat_ref, out_ref):
-    early = early_ref.shape[1]
-    out_ref[:, :early] = early_ref[...]
+def final_kernel(early_ref, last_ref, mass_ref, stat_ref, out_ref, late_ref, sems):
+    early, late = early_ref.shape[1], late_ref.shape[1]
+    ready = pltpu.make_async_copy(early_ref, out_ref.at[:, pl.ds(0, early)], sems.at[0])
+    ready.start()
     part = mass_ref[...], stat_ref[0:1, :], stat_ref[1:2, :]
-    out_ref[:, early:] = logged(*joined(*part, read_message(last_ref)))
+    late_ref[...] = logged(*joined(*part, read_message(last_ref)))
+    rest = pltpu.make_async_copy(late_ref, out_ref.at[:, pl.ds(early, late)], sems.at[1])
+    rest.start()
+    ready.wait()
+    rest.wait()
 
 
 def fits(queries, references, labels):
@@ -374,9 +380,14 @@
         [VMEM] * 5,
         0,
     )(near, lasts[0], *kept, stat)
-    (out,) = call(final_kernel, [((LANES, classes), F32)], [VMEM] * 4, 0)(
-        early, lasts[1], mass, near_stat
-    )
+    (out,) = call(
+        final_kernel,
+        [((LANES, classes), F32)],
+        [VMEM] * 4,
+        0,
+        pl.BlockSpec(memory_space=pltpu.HBM),
+        [pltpu.VMEM((LANES, heights[1]), F32), pltpu.SemaphoreType.DMA((2,))],
+    )(early, lasts[1], mass, near_stat)
     return out
 
 

time: 45.6 us -> 45.6 us (level)
  no operation moved by 1% of the time
where the time goes in v5:
time: 45.6 us; the launch traced here: 45.4 us
  waiting for transfers between devices  23.8 us (52%)
  starting transfers between devices  14.8 us (32%)
  Pallas kernels  4.57 us (10%)
  local copies, waits for them, and re-layouts  2.18 us (5%)
    ppermute x14, waiting for transfers between devices, swapped(): lax.ppermute(value, axis, [(i, i ^ bit) for i in range(lax.axis_size(axis...  23.8 us
    ppermute x14, starting transfers between devices, swapped(): lax.ppermute(value, axis, [(i, i ^ bit) for i in range(lax.axis_size(axis...  14.8 us
    unnamed x6, local copies, waits for them, and re-layouts  2.18 us
    pallas_call x1, Pallas kernels, exchanged(): call(own_kernel, [((height, rows), F32) for height in heights] + [((8, ro...  1.42 us
    pallas_call x2, Pallas kernels, exchanged(): call(far_kernel, [((count, rows), BF16), stat_shape], [VMEM] * 3, score_f...  1.26 us
  transfers between devices with their start and end apart: 14, of which 6 were waited for; matrix products, arithmetic and copies ran while one was open for 0% of the time, Pallas kernels for 8%

profile of v5, /device:TPU:0, one launch (start us, length us, event | category | flops | bytes accessed | tf_op | source)
XLA Modules:
  0.0 45.4 jit_solution(10352031375665517606)
XLA Ops:
  0.0 3.0 %collective-permute-start.2 = (bf16[256,1024]{1,0:T(8,128)(2,1)}, bf16[256,1024]{1,0:T(8,128)(2,1)S(1)}, u32[]{:S(2)}, u32[]{:S(2)}) collective-permute-start(bf16[256,1024]{1,0:T(8,128)(2,1)} %refs_a.1), channel_id=1, source_target_pairs={{0,8},{4,12},{8,0},{12,4},{1,9},{5,13},{9,1},{13,5},{2,10},{6,14},... | collective-permute-start | bytes 1572872 | tf_op jit(solution)/shard_map/ppermute | solution.py:106
  3.0 12.1 %collective-permute-done.2.refs_ref = bf16[256,1024]{1,0:T(8,128)(2,1)S(1)} collective-permute-done((bf16[256,1024]{1,0:T(8,128)(2,1)}, bf16[256,1024]{1,0:T(8,128)(2,1)S(1)}, u32[]{:S(2)}, u32[]{:S(2)}) %collective-permute-start.2) | collective-permute-done | bytes 524320 | tf_op jit(solution)/shard_map/ppermute | solution.py:106
  15.1 1.2 %copy-done = bf16[512,1024]{1,0:T(8,128)(2,1)S(1)} copy-done((bf16[512,1024]{1,0:T(8,128)(2,1)S(1)}, bf16[512,1024]{1,0:T(8,128)(2,1)}, u32[]{:S(2)}) %copy-start) | copy-done | bytes 1048600
  16.4 0.9 %copy-done.1 = bf16[256,512]{1,0:T(8,128)(2,1)S(1)} copy-done((bf16[256,512]{1,0:T(8,128)(2,1)S(1)}, bf16[256,512]{1,0:T(8,128)(2,1)}, u32[]{:S(2)}) %copy-start.1) | copy-done | bytes 262168
  17.4 0.6 %collective-permute-start.4 = (bf16[256,256]{1,0:T(8,128)(2,1)S(1)}, bf16[256,256]{1,0:T(8,128)(2,1)S(1)}, u32[]{:S(2)}, u32[]{:S(2)}) collective-permute-start(bf16[256,256]{1,0:T(8,128)(2,1)S(1)} %get-tuple-element.28.refs_0_), channel_id=1, source_target_pairs={{0,4},{4,0},{8,12},{12,8},{1,5},{5,1},{9,13},{13,9},{2,6},{6,2},{1... | collective-permute-start | bytes 393224 | tf_op jit(solution)/shard_map/ppermute | solution.py:106
  18.0 1.7 %collective-permute-start.7 = (bf16[256,256]{1,0:T(8,128)(2,1)S(1)}, bf16[256,256]{1,0:T(8,128)(2,1)S(1)}, u32[]{:S(2)}, u32[]{:S(2)}) collective-permute-start(bf16[256,256]{1,0:T(8,128)(2,1)S(1)} %get-tuple-element.28.refs_0_), channel_id=1, source_target_pairs={{0,8},{4,12},{8,0},{12,4},{1,9},{5,13},{9,1},{13,5},{2,10},{6,14},... | collective-permute-start | bytes 393224 | tf_op jit(solution)/shard_map/ppermute | solution.py:106
  19.7 0.3 collective-permute-start
  20.0 4.3 %collective-permute-done.7.refs_0_ = bf16[256,256]{1,0:T(8,128)(2,1)S(1)} collective-permute-done((bf16[256,256]{1,0:T(8,128)(2,1)S(1)}, bf16[256,256]{1,0:T(8,128)(2,1)S(1)}, u32[]{:S(2)}, u32[]{:S(2)}) %collective-permute-start.7) | collective-permute-done | bytes 131104 | tf_op jit(solution)/shard_map/ppermute | solution.py:106
  24.4 1.9 %collective-permute-done.refs_0_ = bf16[256,256]{1,0:T(8,128)(2,1)S(1)} collective-permute-done((bf16[256,256]{1,0:T(8,128)(2,1)S(1)}, bf16[256,256]{1,0:T(8,128)(2,1)S(1)}, u32[]{:S(2)}, u32[]{:S(2)}) %collective-permute-start) | collective-permute-done | bytes 131104 | tf_op jit(solution)/shard_map/ppermute | solution.py:106
  26.3 1.4 %shard_map.38 = (f32[256,512]{1,0:T(8,128)S(1)}, f32[256,512]{1,0:T(8,128)S(1)}, f32[8,512]{1,0:T(8,128)S(1)}) custom-call(bf16[512,1024]{1,0:T(8,128)(2,1)S(1)} %get-tuple-element.27.queries_ref, bf16[256,1024]{1,0:T(8,128)(2,1)S(1)} %copy-done.2, bf16[256,1024]{1,0:T(8,128)(2,1)S(1)} %collective-permute-done.3.refs_b, ...), custom_call_target="tpu_custom_call" | custom-call | flops 1073741824 | bytes 1064960 | tf_op jit(solution)/shard_map/pallas_call | solution.py:329
  27.7 0.6 %shard_map.39 = (bf16[256,512]{1,0:T(8,128)(2,1)S(1)}, f32[8,512]{1,0:T(8,128)S(1)}) custom-call(bf16[512,1024]{1,0:T(8,128)(2,1)S(1)} %get-tuple-element.27.queries_ref, bf16[256,1024]{1,0:T(8,128)(2,1)S(1)} %collective-permute-done.2.refs_ref, f32[8,512]{1,0:T(8,128)S(1)} %get-tuple-element.29.stat_ref), custom_call_target="tpu_custom_call" | custom-call | flops 268435456 | bytes 278528 | tf_op jit(solution)/shard_map/pallas_call | solution.py:338
  28.4 0.6 %shard_map.40 = (bf16[256,512]{1,0:T(8,128)(2,1)S(1)}, f32[8,512]{1,0:T(8,128)S(1)}) custom-call(bf16[512,1024]{1,0:T(8,128)(2,1)S(1)} %get-tuple-element.27.queries_ref, bf16[256,1024]{1,0:T(8,128)(2,1)S(1)} %collective-permute-done.6.refs_ref, f32[8,512]{1,0:T(8,128)S(1)} %get-tuple-element.31.stat_ref.refs_5_), custom_call_target="tpu_custom_call" | custom-call | flops 268435456 | bytes 278528 | tf_op jit(solution)/shard_map/pallas_call | solution.py:341
  29.0 0.3 shard_map.41
  29.4 1.9 %collective-permute-start.10 = (bf16[272,128]{1,0:T(8,128)(2,1)S(1)}, bf16[272,128]{1,0:T(8,128)(2,1)S(1)}, u32[]{:S(2)}, u32[]{:S(2)}) collective-permute-start(bf16[272,128]{1,0:T(8,128)(2,1)S(1)} %get-tuple-element.38), channel_id=1, source_target_pairs={{0,1},{1,0},{2,3},{3,2},{4,5},{5,4},{6,7},{7,6},{8,9},{9,8},{10,11... | collective-permute-start | bytes 208904 | tf_op jit(solution)/shard_map/ppermute | solution.py:106
  31.2 0.3 shard_map.42
  31.6 0.3 collective-permute-start.12
  31.9 1.8 %collective-permute-start.9 = (bf16[528,128]{1,0:T(8,128)(2,1)S(1)}, bf16[528,128]{1,0:T(8,128)(2,1)S(1)}, u32[]{:S(2)}, u32[]{:S(2)}) collective-permute-start(bf16[528,128]{1,0:T(8,128)(2,1)S(1)} %get-tuple-element.37), channel_id=1, source_target_pairs={{0,1},{1,0},{2,3},{3,2},{4,5},{5,4},{6,7},{7,6},{8,9},{9,8},{10,11... | collective-permute-start | bytes 405512 | tf_op jit(solution)/shard_map/ppermute | solution.py:106
  33.7 0.4 collective-permute-done.10.received_ref
  34.1 2.8 %collective-permute-start.11 = (bf16[272,128]{1,0:T(8,128)(2,1)S(1)}, bf16[272,128]{1,0:T(8,128)(2,1)S(1)}, u32[]{:S(2)}, u32[]{:S(2)}) collective-permute-start(bf16[272,128]{1,0:T(8,128)(2,1)S(1)} %shard_map.43), channel_id=1, source_target_pairs={{0,2},{1,3},{2,0},{3,1},{4,6},{5,7},{6,4},{7,5},{8,10},{9,11},{10,... | collective-permute-start | bytes 208904 | tf_op jit(solution)/shard_map/ppermute | solution.py:106
  37.0 2.4 %collective-permute-start.13 = (bf16[272,128]{1,0:T(8,128)(2,1)S(1)}, bf16[272,128]{1,0:T(8,128)(2,1)S(1)}, u32[]{:S(2)}, u32[]{:S(2)}) collective-permute-start(bf16[272,128]{1,0:T(8,128)(2,1)S(1)} %shard_map.45), channel_id=1, source_target_pairs={{0,2},{1,3},{2,0},{3,1},{4,6},{5,7},{6,4},{7,5},{8,10},{9,11},{10,... | collective-permute-start | bytes 208904 | tf_op jit(solution)/shard_map/ppermute | solution.py:106
  39.4 1.4 %collective-permute-done.9.near_ref = bf16[528,128]{1,0:T(8,128)(2,1)S(1)} collective-permute-done((bf16[528,128]{1,0:T(8,128)(2,1)S(1)}, bf16[528,128]{1,0:T(8,128)(2,1)S(1)}, u32[]{:S(2)}, u32[]{:S(2)}) %collective-permute-start.9) | collective-permute-done | bytes 135200 | tf_op jit(solution)/shard_map/ppermute | solution.py:106
  40.8 0.2 shard_map.44
  41.0 3.6 %collective-permute-done.13.last_ref = bf16[272,128]{1,0:T(8,128)(2,1)S(1)} collective-permute-done((bf16[272,128]{1,0:T(8,128)(2,1)S(1)}, bf16[272,128]{1,0:T(8,128)(2,1)S(1)}, u32[]{:S(2)}, u32[]{:S(2)}) %collective-permute-start.13) | collective-permute-done | bytes 69664 | tf_op jit(solution)/shard_map/ppermute | solution.py:106
  44.6 0.8 %shard_map.46 = f32[128,512]{1,0:T(8,128)} custom-call(f32[128,256]{1,0:T(8,128)S(1)} %get-tuple-element.42.early_ref, bf16[272,128]{1,0:T(8,128)(2,1)S(1)} %collective-permute-done.13.last_ref, f32[256,128]{1,0:T(8,128)S(1)} %get-tuple-element.45.mass_ref, f32[8,128]{1,0:T(8,128)S(1)} %get-tuple-element.46.stat_ref), custom_call_target="tpu_custom_call" | custom-call | bytes 262144 | tf_op jit(solution)/shard_map/pallas_call | solution.py:383
  (20 shorter events, 0.3 us)
Async XLA Ops:
  0.0 15.1 %collective-permute-start.2 = (bf16[256,1024]{1,0:T(8,128)(2,1)}, bf16[256,1024]{1,0:T(8,128)(2,1)S(1)}, u32[]{:S(2)}, u32[]{:S(2)}) collective-permute-start(bf16[256,1024]{1,0:T(8,128)(2,1)} %refs_a.1), channel_id=1, source_target_pairs={{0,8},{4,12},{8,0},{12,4},{1,9},{5,13},{9,1},{13,5},{2,10},{6,14},... | collective-permute-start | bytes 1572872 | tf_op jit(solution)/shard_map/ppermute | solution.py:106
  3.0 23.3 %collective-permute-start.3 = (bf16[256,1024]{1,0:T(8,128)(2,1)}, bf16[256,1024]{1,0:T(8,128)(2,1)S(1)}, u32[]{:S(2)}, u32[]{:S(2)}) collective-permute-start(bf16[256,1024]{1,0:T(8,128)(2,1)} %refs_a.1), channel_id=1, source_target_pairs={{0,4},{4,0},{8,12},{12,8},{1,5},{5,1},{9,13},{13,9},{2,6},{6,2},{1... | collective-permute-start | bytes 1572872 | tf_op jit(solution)/shard_map/ppermute | solution.py:106
  15.1 13.3 %collective-permute-start.6 = (bf16[256,1024]{1,0:T(8,128)(2,1)S(1)}, bf16[256,1024]{1,0:T(8,128)(2,1)S(1)}, u32[]{:S(2)}, u32[]{:S(2)}) collective-permute-start(bf16[256,1024]{1,0:T(8,128)(2,1)S(1)} %collective-permute-done.2.refs_ref), channel_id=1, source_target_pairs={{0,4},{4,0},{8,12},{12,8},{1,5},{5,1},{9,13},{13,9},{2,6},{6,2},{1... | collective-permute-start | bytes 1572872 | tf_op jit(solution)/shard_map/ppermute | solution.py:106
  15.1 1.2 %copy-start = (bf16[512,1024]{1,0:T(8,128)(2,1)S(1)}, bf16[512,1024]{1,0:T(8,128)(2,1)}, u32[]{:S(2)}) copy-start(bf16[512,1024]{1,0:T(8,128)(2,1)} %queries_ref.1) | copy-start | bytes 3145732
  16.4 0.9 %copy-start.1 = (bf16[256,512]{1,0:T(8,128)(2,1)S(1)}, bf16[256,512]{1,0:T(8,128)(2,1)}, u32[]{:S(2)}) copy-start(bf16[256,512]{1,0:T(8,128)(2,1)} %labels_ref.1) | copy-start | bytes 786436
  17.3 9.0 %copy-start.2 = (bf16[256,1024]{1,0:T(8,128)(2,1)S(1)}, bf16[256,1024]{1,0:T(8,128)(2,1)}, u32[]{:S(2)}) copy-start(bf16[256,1024]{1,0:T(8,128)(2,1)} %refs_a.1) | copy-start | bytes 1572868
  17.4 2.6 %collective-permute-start.4 = (bf16[256,256]{1,0:T(8,128)(2,1)S(1)}, bf16[256,256]{1,0:T(8,128)(2,1)S(1)}, u32[]{:S(2)}, u32[]{:S(2)}) collective-permute-start(bf16[256,256]{1,0:T(8,128)(2,1)S(1)} %get-tuple-element.28.refs_0_), channel_id=1, source_target_pairs={{0,4},{4,0},{8,12},{12,8},{1,5},{5,1},{9,13},{13,9},{2,6},{6,2},{1... | collective-permute-start | bytes 393224 | tf_op jit(solution)/shard_map/ppermute | solution.py:106
  18.0 6.4 %collective-permute-start.7 = (bf16[256,256]{1,0:T(8,128)(2,1)S(1)}, bf16[256,256]{1,0:T(8,128)(2,1)S(1)}, u32[]{:S(2)}, u32[]{:S(2)}) collective-permute-start(bf16[256,256]{1,0:T(8,128)(2,1)S(1)} %get-tuple-element.28.refs_0_), channel_id=1, source_target_pairs={{0,8},{4,12},{8,0},{12,4},{1,9},{5,13},{9,1},{13,5},{2,10},{6,14},... | collective-permute-start | bytes 393224 | tf_op jit(solution)/shard_map/ppermute | solution.py:106
  19.7 6.5 %collective-permute-start = (bf16[256,256]{1,0:T(8,128)(2,1)S(1)}, bf16[256,256]{1,0:T(8,128)(2,1)S(1)}, u32[]{:S(2)}, u32[]{:S(2)}) collective-permute-start(bf16[256,256]{1,0:T(8,128)(2,1)S(1)} %get-tuple-element.26.refs_1_), channel_id=1, source_target_pairs={{0,8},{4,12},{8,0},{12,4},{1,9},{5,13},{9,1},{13,5},{2,10},{6,14},... | collective-permute-start | bytes 393224 | tf_op jit(solution)/shard_map/ppermute | solution.py:106
  20.0 6.3 %collective-permute-start.5 = (bf16[256,256]{1,0:T(8,128)(2,1)S(1)}, bf16[256,256]{1,0:T(8,128)(2,1)S(1)}, u32[]{:S(2)}, u32[]{:S(2)}) collective-permute-start(bf16[256,256]{1,0:T(8,128)(2,1)S(1)} %get-tuple-element.26.refs_1_), channel_id=1, source_target_pairs={{0,4},{4,0},{8,12},{12,8},{1,5},{5,1},{9,13},{13,9},{2,6},{6,2},{1... | collective-permute-start | bytes 393224 | tf_op jit(solution)/shard_map/ppermute | solution.py:106
  24.4 4.6 %collective-permute-start.8 = (bf16[256,256]{1,0:T(8,128)(2,1)S(1)}, bf16[256,256]{1,0:T(8,128)(2,1)S(1)}, u32[]{:S(2)}, u32[]{:S(2)}) collective-permute-start(bf16[256,256]{1,0:T(8,128)(2,1)S(1)} %collective-permute-done.7.refs_0_), channel_id=1, source_target_pairs={{0,4},{4,0},{8,12},{12,8},{1,5},{5,1},{9,13},{13,9},{2,6},{6,2},{1... | collective-permute-start | bytes 393224 | tf_op jit(solution)/shard_map/ppermute | solution.py:106
  26.3 4.9 %collective-permute-start.1 = (bf16[256,256]{1,0:T(8,128)(2,1)S(1)}, bf16[256,256]{1,0:T(8,128)(2,1)S(1)}, u32[]{:S(2)}, u32[]{:S(2)}) collective-permute-start(bf16[256,256]{1,0:T(8,128)(2,1)S(1)} %collective-permute-done.refs_0_), channel_id=1, source_target_pairs={{0,4},{4,0},{8,12},{12,8},{1,5},{5,1},{9,13},{13,9},{2,6},{6,2},{1... | collective-permute-start | bytes 393224 | tf_op jit(solution)/shard_map/ppermute | solution.py:106
  29.4 4.7 %collective-permute-start.10 = (bf16[272,128]{1,0:T(8,128)(2,1)S(1)}, bf16[272,128]{1,0:T(8,128)(2,1)S(1)}, u32[]{:S(2)}, u32[]{:S(2)}) collective-permute-start(bf16[272,128]{1,0:T(8,128)(2,1)S(1)} %get-tuple-element.38), channel_id=1, source_target_pairs={{0,1},{1,0},{2,3},{3,2},{4,5},{5,4},{6,7},{7,6},{8,9},{9,8},{10,11... | collective-permute-start | bytes 208904 | tf_op jit(solution)/shard_map/ppermute | solution.py:106
  31.6 5.4 %collective-permute-start.12 = (bf16[272,128]{1,0:T(8,128)(2,1)S(1)}, bf16[272,128]{1,0:T(8,128)(2,1)S(1)}, u32[]{:S(2)}, u32[]{:S(2)}) collective-permute-start(bf16[272,128]{1,0:T(8,128)(2,1)S(1)} %get-tuple-element.43), channel_id=1, source_target_pairs={{0,1},{1,0},{2,3},{3,2},{4,5},{5,4},{6,7},{7,6},{8,9},{9,8},{10,11... | collective-permute-start | bytes 208904 | tf_op jit(solution)/shard_map/ppermute | solution.py:106
  31.9 9.0 %collective-permute-start.9 = (bf16[528,128]{1,0:T(8,128)(2,1)S(1)}, bf16[528,128]{1,0:T(8,128)(2,1)S(1)}, u32[]{:S(2)}, u32[]{:S(2)}) collective-permute-start(bf16[528,128]{1,0:T(8,128)(2,1)S(1)} %get-tuple-element.37), channel_id=1, source_target_pairs={{0,1},{1,0},{2,3},{3,2},{4,5},{5,4},{6,7},{7,6},{8,9},{9,8},{10,11... | collective-permute-start | bytes 405512 | tf_op jit(solution)/shard_map/ppermute | solution.py:106
  34.1 6.7 %collective-permute-start.11 = (bf16[272,128]{1,0:T(8,128)(2,1)S(1)}, bf16[272,128]{1,0:T(8,128)(2,1)S(1)}, u32[]{:S(2)}, u32[]{:S(2)}) collective-permute-start(bf16[272,128]{1,0:T(8,128)(2,1)S(1)} %shard_map.43), channel_id=1, source_target_pairs={{0,2},{1,3},{2,0},{3,1},{4,6},{5,7},{6,4},{7,5},{8,10},{9,11},{10,... | collective-permute-start | bytes 208904 | tf_op jit(solution)/shard_map/ppermute | solution.py:106
  37.0 7.5 %collective-permute-start.13 = (bf16[272,128]{1,0:T(8,128)(2,1)S(1)}, bf16[272,128]{1,0:T(8,128)(2,1)S(1)}, u32[]{:S(2)}, u32[]{:S(2)}) collective-permute-start(bf16[272,128]{1,0:T(8,128)(2,1)S(1)} %shard_map.45), channel_id=1, source_target_pairs={{0,2},{1,3},{2,0},{3,1},{4,6},{5,7},{6,4},{7,5},{8,10},{9,11},{10,... | collective-permute-start | bytes 208904 | tf_op jit(solution)/shard_map/ppermute | solution.py:106
